TPU v7x, 32 devices: a whole 2x2x4 slice. The times are simulated.
32 devices in a mesh: dp: 8 (over z, x), tensor: 4 (over y, core).
Axes of the slice: x: 2, y: 2, z: 4, core: 2. Of those that a mesh axis runs over, the one named last changes fastest.
Arguments:
- tokens: bfloat16 [8192, 640], P('dp'), may hold values from -6 to 6
- segment_ids: int32 [8, 1024], P('dp'), may hold values from 0 to 3, never falling along the last dimension, each value on 1 to 768 neighbouring positions
- input_gain: float32 [640], replicated, may hold values from -0.5 to 0.5
- q_weight: bfloat16 [640, 1024], P(None, 'tensor'), as said below
- k_weight: bfloat16 [640, 256], replicated, as said below
- v_weight: bfloat16 [640, 256], replicated, may hold values from -0.25 to 0.25
- query_gain: float32 [256], replicated, as said below
- key_gain: float32 [256], replicated, as said below
- o_weight: bfloat16 [640, 1024], P(None, 'tensor'), may hold values from -0.1875 to 0.1875
- post_attn_gain: float32 [640], replicated, may hold values from -0.5 to 0.5
- pre_ffn_gain: float32 [640], replicated, may hold values from -0.5 to 0.5
- gate_weight: bfloat16 [640, 2048], P(None, 'tensor'), may hold values from -0.25 to 0.25
- up_weight: bfloat16 [640, 2048], P(None, 'tensor'), may hold values from -0.25 to 0.25
- down_weight: bfloat16 [640, 2048], P(None, 'tensor'), may hold values from -0.125 to 0.125
- post_ffn_gain: float32 [640], replicated, may hold values from -0.5 to 0.5
- out_grad: bfloat16 [8192, 640], P('dp'), may hold values from -6 to 6
Outputs:
- output: bfloat16 [8192, 640], P('dp')
- grad_tokens: float32 [8192, 640], P('dp')
- grad_input_gain: float32 [640], replicated
- grad_q_weight: float32 [640, 1024], P('dp', 'tensor')
- grad_k_weight: float32 [640, 256], P('dp')
- grad_v_weight: float32 [640, 256], P('dp')
- grad_query_gain: float32 [256], replicated
- grad_key_gain: float32 [256], replicated
- grad_o_weight: float32 [640, 1024], P('dp', 'tensor')
- grad_post_attn_gain: float32 [640], replicated
- grad_pre_ffn_gain: float32 [640], replicated
- grad_gate_weight: float32 [640, 2048], P('dp', 'tensor')
- grad_up_weight: float32 [640, 2048], P('dp', 'tensor')
- grad_down_weight: float32 [640, 2048], P('dp', 'tensor')
- grad_post_ffn_gain: float32 [640], replicated
Inputs may be any that keep to these rules, and one draw needn't show every extreme that they name: `segment_ids`: along each row numbers never fall; a run of equal numbers is one document. `q_weight`: entries lie within -0.25 to 0.25. `k_weight`: entries lie within -0.25 to 0.25. `query_gain`: entries lie within -0.5 to 2.5. `key_gain`: entries lie within -0.5 to 2.5.
All inputs are finite; a program needn't handle non-finite values.
Results may differ from a plain program's by a relative error of at most 0.034.
The roundings to bfloat16 on the way count: a program that leaves them out, or rounds other values in their place, can miss the bound.
Values may be sent and summed in bfloat16 or wider, within the bound.
A program may use at most 128 MiB of HBM per device.

v0:
```python
import functools

import jax
import jax.numpy as jnp
from jax import lax
from jax.experimental import pallas as pl
from jax.experimental.pallas import tpu as pltpu
from jax.sharding import PartitionSpec as P

WIN = 512
ROWS = 256


norm_eps = 1e-06
rope_base = 10000.0
gelu_coef = 0.7978845608028654
cube_coef = 0.044715
masked_value = -1e30
contract_rows = (((0,), (0,)), ((), ()))
contract_cols = (((1,), (1,)), ((), ()))
F32 = jnp.float32
BF16 = jnp.bfloat16


def mat(left, right):
    return jnp.dot(left, right, preferred_element_type=F32)


def mat_rows(left, right):
    return lax.dot_general(left, right, contract_rows, preferred_element_type=F32)


def mat_cols(left, right):
    return lax.dot_general(left, right, contract_cols, preferred_element_type=F32)


def rms_unit(values):
    inverse = lax.rsqrt(jnp.mean(values * values, axis=-1, keepdims=True) + norm_eps)
    return (values * inverse, inverse)


def rms_backward(grad_vals, unit_vals, inverse, gain_vec):
    scaled = grad_vals * (1.0 + gain_vec)
    return inverse * (scaled - unit_vals * jnp.mean(scaled * unit_vals, axis=-1, keepdims=True))


def rotate(values, cosine, sine_tab, sign):
    half_dim = values.shape[-1] // 2
    first = values[:, :half_dim]
    second = values[:, half_dim:]
    return jnp.concatenate(
        [first * cosine - sign * second * sine_tab, second * cosine + sign * first * sine_tab],
        axis=-1,
    )


def column_sum(values):
    return jnp.sum(values, axis=0, keepdims=True)


def allowed_keys(low_col, block):
    rows = low_col.shape[0]
    col_ids = lax.broadcasted_iota(jnp.int32, (rows, rows + WIN), 1) - WIN
    row_ids = lax.broadcasted_iota(jnp.int32, (rows, rows + WIN), 0)
    return (col_ids >= low_col - block * rows) & (col_ids <= row_ids)


def attend_kernel(
    tok, gain, q_w, k_w, v_w, q_gain, k_gain, o_w, cosine, sine_tab, low,
    term, attn, q_rot, k_pad, v_pad, stats, q_unit, k_unit,
):
    block = pl.program_id(0)
    rows, head_dim = attn.shape

    @pl.when(block == 0)
    def _():
        k_pad[:WIN, :] = jnp.zeros((WIN, head_dim), BF16)
        v_pad[:WIN, :] = jnp.zeros((WIN, head_dim), BF16)

    unit_in, _ = rms_unit(tok[...].astype(F32))
    normed = (unit_in * (1.0 + gain[...])).astype(BF16)
    cos_b, sin_b = cosine[...], sine_tab[...]
    q_u, q_inv = rms_unit(mat(normed, q_w[...]))
    k_u, k_inv = rms_unit(mat(normed, k_w[...]))
    q_unit[...] = q_u
    k_unit[...] = k_u
    q_r = rotate(q_u * (1.0 + q_gain[...]), cos_b, sin_b, 1.0).astype(BF16)
    q_rot[...] = q_r
    here = pl.ds(pl.multiple_of(block * rows + WIN, rows), rows)
    span = pl.ds(pl.multiple_of(block * rows, rows), rows + WIN)
    k_pad[here, :] = rotate(k_u * (1.0 + k_gain[...]), cos_b, sin_b, 1.0).astype(BF16)
    v_pad[here, :] = mat(normed, v_w[...]).astype(BF16)
    scores = mat_cols(q_r, k_pad[span, :]) * (head_dim ** (-0.5))
    scores = jnp.where(allowed_keys(low[...], block), scores, masked_value)
    row_max = jnp.max(scores, axis=-1, keepdims=True)
    exp_vals = jnp.exp(scores - row_max)
    row_total = jnp.sum(exp_vals, axis=-1, keepdims=True)
    probs = (exp_vals * (1.0 / row_total)).astype(BF16)
    result = mat(probs, v_pad[span, :]).astype(BF16)
    attn[...] = result
    term[...] = mat_cols(result, o_w[...]).astype(BF16)
    lane = lax.broadcasted_iota(jnp.int32, stats.shape, 1)
    lse = row_max + jnp.log(row_total)
    stats[...] = jnp.where(lane == 0, lse, jnp.where(lane == 1, q_inv, k_inv))


def middle(tok, attn_sum, post_attn_gain):
    attn_unit, attn_inv = rms_unit(attn_sum[...].astype(F32))
    hidden = tok[...].astype(F32) + attn_unit * (1.0 + post_attn_gain[...])
    mid_unit, mid_inv = rms_unit(hidden)
    return (attn_unit, attn_inv, hidden, mid_unit, mid_inv)


def ffn_kernel(tok, attn_sum, pa_gain, pre_gain, gate_w, up_w, down_w, term, gate, up):
    _, _, _, mid_unit, _ = middle(tok, attn_sum, pa_gain)
    normed = (mid_unit * (1.0 + pre_gain[...])).astype(BF16)
    gate_pre = mat(normed, gate_w[...])
    up_pre = mat(normed, up_w[...])
    gate[...] = gate_pre
    up[...] = up_pre
    tanh_val = jnp.tanh(gelu_coef * (gate_pre + cube_coef * gate_pre * gate_pre * gate_pre))
    act = (0.5 * gate_pre * (1.0 + tanh_val) * up_pre).astype(BF16)
    term[...] = mat_cols(act, down_w[...]).astype(BF16)


def ffn_back_kernel(
    tok, attn_sum, ffn_sum, out_grad, gate, up, pa_gain, pre_gain, pf_gain, gate_w, up_w, down_w,
    output, term, weight_grads, gains, total,
):
    block = pl.program_id(0)

    @pl.when(block == 0)
    def _():
        total[...] = jnp.zeros_like(total)
        gains[...] = jnp.zeros_like(gains)

    _, _, hidden, mid_unit, mid_inv = middle(tok, attn_sum, pa_gain)
    normed = (mid_unit * (1.0 + pre_gain[...])).astype(BF16)
    ffn_unit, ffn_inv = rms_unit(ffn_sum[...].astype(F32))
    output[...] = (hidden + ffn_unit * (1.0 + pf_gain[...])).astype(BF16)
    grad_out = out_grad[...].astype(F32)
    gains[0:1, :] += column_sum(grad_out * ffn_unit)
    grad_sum = rms_backward(grad_out, ffn_unit, ffn_inv, pf_gain[...]).astype(BF16)
    grad_act = mat(grad_sum, down_w[...])
    gate_pre, up_pre = gate[...], up[...]
    squared = gate_pre * gate_pre
    tanh_val = jnp.tanh(gelu_coef * (gate_pre + cube_coef * squared * gate_pre))
    gelu_value = 0.5 * gate_pre * (1.0 + tanh_val)
    slope = 0.5 * (1.0 + tanh_val) + 0.5 * gate_pre * (1.0 - tanh_val * tanh_val) * gelu_coef * (
        1.0 + 3.0 * cube_coef * squared
    )
    act = (gelu_value * up_pre).astype(BF16)
    grad_gate = (grad_act * up_pre * slope).astype(BF16)
    grad_up = (grad_act * gelu_value).astype(BF16)
    units = gate_pre.shape[1]
    total[:, :units] += mat_rows(normed, grad_gate)
    total[:, units : 2 * units] += mat_rows(normed, grad_up)
    total[:, 2 * units :] += mat_rows(grad_sum, act)
    grad_mid = mat_cols(grad_gate, gate_w[...]) + mat_cols(grad_up, up_w[...])
    gains[1:2, :] += column_sum(grad_mid * mid_unit)
    term[...] = rms_backward(grad_mid, mid_unit, mid_inv, pre_gain[...]).astype(BF16)

    @pl.when(block == pl.num_programs(0) - 1)
    def _():
        weight_grads[...] = total[...].astype(BF16)


def attend_back_kernel(
    tok, out_grad, ffn_back, attn_sum, attn, q_rot, stats, q_unit, k_unit, cosine, sine_tab, low,
    k_pad, v_pad, pa_gain, in_gain, q_gain, k_gain, q_w, k_w, v_w, o_w,
    term, weight_grads, gains, head_gains, total, grad_k, grad_v,
):
    step = pl.program_id(0)
    block = pl.num_programs(0) - 1 - step
    rows, head_dim = attn.shape
    scale = head_dim ** (-0.5)

    @pl.when(step == 0)
    def _():
        for ref in (total, gains, head_gains, grad_k, grad_v):
            ref[...] = jnp.zeros_like(ref)

    attn_unit, attn_inv = rms_unit(attn_sum[...].astype(F32))
    grad_hidden = out_grad[...].astype(F32) + ffn_back[...].astype(F32)
    gains[0:1, :] += column_sum(grad_hidden * attn_unit)
    grad_sum = rms_backward(grad_hidden, attn_unit, attn_inv, pa_gain[...]).astype(BF16)
    grad_attn = mat(grad_sum, o_w[...]).astype(BF16)
    attn_vals = attn[...]
    total[:, :head_dim] += mat_rows(grad_sum, attn_vals)
    delta = jnp.sum(grad_attn.astype(F32) * attn_vals.astype(F32), axis=-1, keepdims=True)
    span = pl.ds(pl.multiple_of(block * rows, rows), rows + WIN)
    here = pl.ds(pl.multiple_of(block * rows + WIN, rows), rows)
    q_r = q_rot[...]
    k_span, v_span = k_pad[span, :], v_pad[span, :]
    scores = mat_cols(q_r, k_span) * scale
    allowed = allowed_keys(low[...], block)
    probs = jnp.exp(jnp.where(allowed, scores - stats[:, 0:1], masked_value))
    grad_probs = mat_cols(grad_attn, v_span)
    grad_scores = (probs * (grad_probs - delta) * scale).astype(BF16)
    grad_query = mat(grad_scores, k_span)
    grad_k[span, :] += mat_rows(grad_scores, q_r)
    grad_v[span, :] += mat_rows(probs.astype(BF16), grad_attn)
    cos_b, sin_b = cosine[...], sine_tab[...]
    grad_q_unit = rotate(grad_query, cos_b, sin_b, -1.0)
    grad_k_unit = rotate(grad_k[here, :], cos_b, sin_b, -1.0)
    q_u, k_u = q_unit[...], k_unit[...]
    head_gains[0:1, :] += column_sum(grad_q_unit * q_u)
    head_gains[1:2, :] += column_sum(grad_k_unit * k_u)
    grad_q_bf = rms_backward(grad_q_unit, q_u, stats[:, 1:2], q_gain[...]).astype(BF16)
    grad_k_bf = rms_backward(grad_k_unit, k_u, stats[:, 2:3], k_gain[...]).astype(BF16)
    grad_v_bf = grad_v[here, :].astype(BF16)
    unit_in, inv_in = rms_unit(tok[...].astype(F32))
    normed = (unit_in * (1.0 + in_gain[...])).astype(BF16)
    total[:, head_dim : 2 * head_dim] += mat_rows(normed, grad_q_bf)
    total[:, 2 * head_dim : 3 * head_dim] += mat_rows(normed, grad_k_bf)
    total[:, 3 * head_dim :] += mat_rows(normed, grad_v_bf)
    grad_in = mat_cols(grad_q_bf, q_w[...]) + mat_cols(grad_k_bf, k_w[...])
    grad_in = grad_in + mat_cols(grad_v_bf, v_w[...])
    gains[1:2, :] += column_sum(grad_in * unit_in)
    term[...] = rms_backward(grad_in, unit_in, inv_in, in_gain[...]).astype(BF16)

    @pl.when(block == 0)
    def _():
        weight_grads[...] = total[...].astype(BF16)


def row_call(kernel, name, steps, row_args, full_args, row_outs, full_outs, scratch, flops, reverse):
    def row_map(i):
        return (steps - 1 - i if reverse else i, 0)

    def full_map(i):
        return (0, 0)

    def row_spec(shape):
        return pl.BlockSpec((shape[0] // steps, shape[1]), row_map)

    def full_spec(shape):
        return pl.BlockSpec(shape, full_map)

    moved = sum(x.size * x.dtype.itemsize for x in tuple(row_args) + tuple(full_args))
    return pl.pallas_call(
        kernel,
        name=name,
        out_shape=tuple(jax.ShapeDtypeStruct(s, d) for s, d in tuple(row_outs) + tuple(full_outs)),
        grid_spec=pltpu.PrefetchScalarGridSpec(
            num_scalar_prefetch=0,
            grid=(steps,),
            in_specs=[row_spec(x.shape) for x in row_args] + [full_spec(x.shape) for x in full_args],
            out_specs=[row_spec(s) for s, _ in row_outs] + [full_spec(s) for s, _ in full_outs],
            scratch_shapes=scratch,
        ),
        compiler_params=pltpu.CompilerParams(
            dimension_semantics=("arbitrary",), vmem_limit_bytes=48 * 1024 * 1024
        ),
        cost_estimate=pl.CostEstimate(flops=flops, bytes_accessed=moved, transcendentals=0),
    )(*row_args, *full_args)


def flip_pairs(size, bit):
    return [(index, index ^ bit) for index in range(size)]


def sum_tensor(term, size):
    rows = term.shape[0]
    half = rows // 2
    low = lax.rem(lax.axis_index("tensor"), 2)
    term = lax.optimization_barrier(term.astype(jnp.bfloat16))
    mine = lax.dynamic_slice_in_dim(term, low * half, half, 0)
    other = lax.dynamic_slice_in_dim(term, (1 - low) * half, half, 0)
    got = lax.ppermute(other, "tensor", flip_pairs(size, 1))
    total = mine.astype(jnp.float32) + got.astype(jnp.float32)
    bit = 2
    while bit < size:
        sent = lax.optimization_barrier(total.astype(jnp.bfloat16))
        got = lax.ppermute(sent, "tensor", flip_pairs(size, bit))
        total = sent.astype(jnp.float32) + got.astype(jnp.float32)
        bit *= 2
    sent = lax.optimization_barrier(total.astype(jnp.bfloat16))
    got = lax.ppermute(sent, "tensor", flip_pairs(size, 1))
    first = jnp.where(low == 0, sent, got)
    second = jnp.where(low == 0, got, sent)
    return jnp.concatenate([first, second], axis=0)


def sum_small(values, size):
    total = values
    bit = 1
    while bit < size:
        sent = lax.optimization_barrier(total.astype(jnp.bfloat16))
        got = lax.ppermute(sent, "tensor", flip_pairs(size, bit))
        total = sent.astype(jnp.float32) + got.astype(jnp.float32)
        bit *= 2
    return total


def scatter_dp(blocks, size):
    index = lax.axis_index("dp")
    rows, cols = blocks.shape[1:]
    total = blocks
    bit = 1
    while bit < size:
        low = lax.rem(lax.div(index, bit), 2)
        parts = total.reshape(-1, 2, rows, cols)
        sent = lax.optimization_barrier(
            lax.dynamic_index_in_dim(parts, 1 - low, 1, keepdims=False).astype(jnp.bfloat16)
        )
        kept = lax.dynamic_index_in_dim(parts, low, 1, keepdims=False)
        got = lax.ppermute(sent, "dp", flip_pairs(size, bit))
        total = kept.astype(jnp.float32) + got.astype(jnp.float32)
        bit *= 2
    return total.reshape(rows, cols)


def on_device(
    tensor_size,
    dp_size,
    tokens,
    segment_ids,
    input_gain,
    q_weight,
    k_weight,
    v_weight,
    query_gain,
    key_gain,
    o_weight,
    post_attn_gain,
    pre_ffn_gain,
    gate_weight,
    up_weight,
    down_weight,
    post_ffn_gain,
    out_grad,
):
    tok_count, model = tokens.shape
    head_dim = k_weight.shape[1]
    units = gate_weight.shape[1]
    steps = tok_count // ROWS
    segments = segment_ids[0]
    row_index = jnp.arange(tok_count, dtype=jnp.int32)
    starts = jnp.sum((segments[None, :] < segments[:, None]).astype(jnp.int32), axis=1, keepdims=True)
    positions = row_index[:, None] - starts
    low = jnp.maximum(starts, row_index[:, None] - (WIN - 1))
    frequency = rope_base ** (-(jnp.arange(head_dim // 2, dtype=F32) * 2.0 / head_dim))
    angles = positions.astype(F32) * frequency[None, :]
    cosine, sine_tab = jnp.cos(angles), jnp.sin(angles)
    in_gain, pa_gain, pre_gain, pf_gain, q_gain, k_gain = (
        g[None, :]
        for g in (input_gain, post_attn_gain, pre_ffn_gain, post_ffn_gain, query_gain, key_gain)
    )
    square = tok_count * model * head_dim
    attend_full = (in_gain, q_weight, k_weight, v_weight, q_gain, k_gain, o_weight)
    wide = (tok_count, model)
    heads = (tok_count, head_dim)
    padded = (tok_count + WIN, head_dim)

    def attend(tok, cos_b, sin_b, low_b, gain, q_w, k_w, v_w, qg, kg, o_w,
               term, attn, q_rot, stats, q_unit, k_unit, k_pad, v_pad):
        attend_kernel(tok, gain, q_w, k_w, v_w, qg, kg, o_w, cos_b, sin_b, low_b,
                      term, attn, q_rot, k_pad, v_pad, stats, q_unit, k_unit)

    term, attn, q_rot, stats, q_unit, k_unit, k_pad, v_pad = row_call(
        attend, "attend", steps, (tokens, cosine, sine_tab, low), attend_full,
        ((wide, BF16), (heads, BF16), (heads, BF16), ((tok_count, 128), F32), (heads, F32), (heads, F32)),
        ((padded, BF16), (padded, BF16)), (), 14 * square, False,
    )
    attn_sum = sum_tensor(term, tensor_size)
    hidden_shape = (tok_count, units)
    term, gate, up = row_call(
        ffn_kernel, "ffn", steps, (tokens, attn_sum),
        (pa_gain, pre_gain, gate_weight, up_weight, down_weight),
        ((wide, BF16), (hidden_shape, F32), (hidden_shape, F32)), (), (), 12 * square, False,
    )
    ffn_sum = sum_tensor(term, tensor_size)
    output, term, early, ffn_gains = row_call(
        ffn_back_kernel, "ffn_back", steps, (tokens, attn_sum, ffn_sum, out_grad, gate, up),
        (pa_gain, pre_gain, pf_gain, gate_weight, up_weight, down_weight),
        ((wide, BF16), (wide, BF16)), (((model, 3 * units), BF16), ((8, model), F32)),
        (pltpu.VMEM((model, 3 * units), F32),), 24 * square, False,
    )
    part_rows = model // dp_size
    early = scatter_dp(early.reshape(dp_size, part_rows, 3 * units), dp_size)
    ffn_back = sum_tensor(term, tensor_size)
    term, late, attn_gains, head_gains = row_call(
        attend_back_kernel, "attend_back", steps,
        (tokens, out_grad, ffn_back, attn_sum, attn, q_rot, stats, q_unit, k_unit, cosine, sine_tab, low),
        (k_pad, v_pad, pa_gain, in_gain, q_gain, k_gain, q_weight, k_weight, v_weight, o_weight),
        ((wide, BF16),), (((model, 4 * head_dim), BF16), ((8, model), F32), ((8, head_dim), F32)),
        (pltpu.VMEM((model, 4 * head_dim), F32), pltpu.VMEM(padded, F32), pltpu.VMEM(padded, F32)),
        30 * square, True,
    )
    attn_back = sum_tensor(term, tensor_size)
    grad_tokens = out_grad.astype(F32) + ffn_back.astype(F32) + attn_back.astype(F32)
    gains = jnp.concatenate(
        [attn_gains[0], ffn_gains[0], attn_gains[1], ffn_gains[1], head_gains[0], head_gains[1]]
    )
    gain_count = gains.shape[0]
    late_cols = 4 * head_dim
    gain_rows = -(-gain_count // (16 * late_cols)) * 16
    gains = jnp.pad(gains, (0, gain_rows * late_cols - gain_count)).reshape(1, gain_rows, late_cols)
    gains = jnp.broadcast_to(gains.astype(BF16), (dp_size, gain_rows, late_cols))
    late = jnp.concatenate([late.reshape(dp_size, part_rows, late_cols), gains], axis=1)
    late = scatter_dp(late, dp_size)
    grad_o_w = late[:part_rows, :head_dim]
    grad_q_w = late[:part_rows, head_dim : 2 * head_dim]
    gain_part = late[part_rows:].reshape(-1)[:gain_count]
    shared = jnp.concatenate(
        [late[:part_rows, 2 * head_dim :], late[part_rows:].reshape(2 * gain_rows, 2 * head_dim)], axis=0
    )
    shared = sum_small(shared, tensor_size)
    grad_k_w = shared[:part_rows, :head_dim]
    grad_v_w = shared[:part_rows, head_dim:]
    gain_sum = shared[part_rows:].reshape(-1)
    grad_post_attn = gain_part[:model]
    grad_post_ffn = gain_part[model : 2 * model]
    grad_input_gain = gain_sum[2 * model : 3 * model]
    grad_pre_ffn = gain_sum[3 * model : 4 * model]
    grad_query_gain = gain_sum[4 * model : 4 * model + head_dim]
    grad_key_gain = gain_sum[4 * model + head_dim : gain_count]
    grad_gate_w = early[:, :units]
    grad_up_w = early[:, units : 2 * units]
    grad_down_w = early[:, 2 * units :]
    return (
        output, grad_tokens, grad_input_gain, grad_q_w, grad_k_w, grad_v_w, grad_query_gain,
        grad_key_gain, grad_o_w, grad_post_attn, grad_pre_ffn, grad_gate_w, grad_up_w, grad_down_w,
        grad_post_ffn,
    )


def solution(mesh):
    in_specs = (
        P("dp", None),
        P("dp", None),
        P(),
        P(None, "tensor"),
        P(),
        P(),
        P(),
        P(),
        P(None, "tensor"),
        P(),
        P(),
        P(None, "tensor"),
        P(None, "tensor"),
        P(None, "tensor"),
        P(),
        P("dp", None),
    )
    out_specs = (
        P("dp", None),
        P("dp", None),
        P(),
        P("dp", "tensor"),
        P("dp", None),
        P("dp", None),
        P(),
        P(),
        P("dp", "tensor"),
        P(),
        P(),
        P("dp", "tensor"),
        P("dp", "tensor"),
        P("dp", "tensor"),
        P(),
    )
    body = functools.partial(on_device, mesh.shape["tensor"], mesh.shape["dp"])
    return jax.shard_map(
        body, mesh=mesh, in_specs=in_specs, out_specs=out_specs, check_vma=False
    )
```

profile of v0, /device:TPU:0, one launch (start us, length us, event | category | flops | bytes accessed | tf_op | source)
XLA Modules:
  0.0 187.3 jit_solution(17171325376680886376)
XLA Ops:
  0.7 1.3 convert_reduce_fusion
  2.1 0.2 copy.34
  2.4 1.9 %multiply_sine_fusion = (f32[1024,128]{1,0:T(8,128)S(1)}, f32[1024,128]{1,0:T(8,128)S(1)}) fusion(f32[128]{0:T(128)S(1)} %negate_power_fusion, f32[1024]{0:T(1024)S(1)} %subtract_convert_fusion), kind=kLoop, calls=%fused_computation.28 | loop fusion | flops 131072 | bytes 1053184 | tf_op jit(solution)/shard_map/sin | solution.py:345
  4.4 8.9 %attend.1 = (bf16[1024,640]{1,0:T(8,128)(2,1)}, bf16[1024,256]{1,0:T(8,128)(2,1)S(1)}, bf16[1024,256]{1,0:T(8,128)(2,1)S(1)}, f32[1024,128]{1,0:T(8,128)S(1)}, f...) custom-call(bf16[1024,640]{1,0:T(8,128)(2,1)} %tok.7, ...), custom_call_target="tpu_custom_call" | custom-call | flops 2348810240 | bytes 3678720 | tf_op jit(solution)/shard_map/attend/pallas_call | solution.py:241
  13.3 0.9 copy-done.18
  14.2 0.8 copy-done.24
  15.0 0.8 copy-done.26
  15.9 2.5 %constant_dynamic-slice_fusion.3 = bf16[512,640]{1,0:T(8,128)(2,1)} fusion(bf16[1024,640]{1,0:T(8,128)(2,1)} %get-tuple-element.34, s32[]{:T(128)S(6)} %select_n.80), kind=kLoop, calls=%fused_computation.54 | loop fusion | bytes 1310724 | tf_op jit(solution)/shard_map/dynamic_slice | solution.py:269
  18.3 0.5 collective-permute-start
  18.8 2.1 %collective-permute-done = bf16[512,640]{1,0:T(8,128)(2,1)} collective-permute-done((bf16[512,640]{1,0:T(8,128)(2,1)}, bf16[512,640]{1,0:T(8,128)(2,1)}, u32[]{:S(2)}, u32[]{:S(2)}) %collective-permute-start) | collective-permute-done | bytes 655392 | tf_op jit(solution)/shard_map/ppermute | solution.py:270
  20.9 1.3 add_convert_fusion.7
  22.2 2.9 %collective-permute-start.1 = (bf16[512,640]{1,0:T(8,128)(2,1)S(1)}, bf16[512,640]{1,0:T(8,128)(2,1)S(1)}, u32[]{:S(2)}, u32[]{:S(2)}) collective-permute-start(bf16[512,640]{1,0:T(8,128)(2,1)S(1)} %add_convert_fusion.7), channel_id=1, source_target_pairs={{0,2},{1,3},{2,0},{3,1},{4,6},{5,7},{6,4},{7,5},{8,10},{9,11},{10,... | collective-permute-start | bytes 1966088 | tf_op jit(solution)/shard_map/ppermute | solution.py:275
  25.2 15.0 %collective-permute-done.1 = bf16[512,640]{1,0:T(8,128)(2,1)S(1)} collective-permute-done((bf16[512,640]{1,0:T(8,128)(2,1)S(1)}, bf16[512,640]{1,0:T(8,128)(2,1)S(1)}, u32[]{:S(2)}, u32[]{:S(2)}) %collective-permute-start.1) | collective-permute-done | bytes 655392 | tf_op jit(solution)/shard_map/ppermute | solution.py:275
  40.5 2.0 %collective-permute-done.2 = bf16[512,640]{1,0:T(8,128)(2,1)S(1)} collective-permute-done((bf16[512,640]{1,0:T(8,128)(2,1)S(1)}, bf16[512,640]{1,0:T(8,128)(2,1)S(1)}, u32[]{:S(2)}, u32[]{:S(2)}) %collective-permute-start.2) | collective-permute-done | bytes 655392 | tf_op jit(solution)/shard_map/ppermute | solution.py:279
  42.8 0.8 copy-done.8
  43.6 0.5 copy-done.5
  44.2 0.2 copy-done.7
  44.5 5.2 %ffn.1 = (bf16[1024,640]{1,0:T(8,128)(2,1)S(1)}, f32[1024,512]{1,0:T(8,128)}, f32[1024,512]{1,0:T(8,128)}) custom-call(bf16[1024,640]{1,0:T(8,128)(2,1)S(1)} %copy-done.5, bf16[1024,640]{1,0:T(8,128)(2,1)S(1)} %pad_maximum_fusion.attn_sum, f32[1,640]{1,0:T(1,128)S(1)} %broadcast_in_dim.30.pa_gain, f32[1,640]{1,0:T(1,128)S(1)} %broadcast_in_dim.31.pre_gain, ...), custom_call_target="tpu_custom_call" | custom-call | flops 2013265920 | bytes 4592640 | tf_op jit(solution)/shard_map/ffn/pallas_call | solution.py:241
  49.7 0.2 collective-permute-start.3
  49.9 2.0 %collective-permute-done.3 = bf16[512,640]{1,0:T(8,128)(2,1)S(1)} collective-permute-done((bf16[512,640]{1,0:T(8,128)(2,1)S(1)}, bf16[512,640]{1,0:T(8,128)(2,1)S(1)}, u32[]{:S(2)}, u32[]{:S(2)}) %collective-permute-start.3) | collective-permute-done | bytes 655392 | tf_op jit(solution)/shard_map/ppermute | solution.py:270
  52.1 1.8 collective-permute-start.4
  53.9 15.0 %collective-permute-done.4 = bf16[512,640]{1,0:T(8,128)(2,1)S(1)} collective-permute-done((bf16[512,640]{1,0:T(8,128)(2,1)S(1)}, bf16[512,640]{1,0:T(8,128)(2,1)S(1)}, u32[]{:S(2)}, u32[]{:S(2)}) %collective-permute-start.4) | collective-permute-done | bytes 655392 | tf_op jit(solution)/shard_map/ppermute | solution.py:275
  69.2 2.1 %collective-permute-done.5 = bf16[512,640]{1,0:T(8,128)(2,1)S(1)} collective-permute-done((bf16[512,640]{1,0:T(8,128)(2,1)S(1)}, bf16[512,640]{1,0:T(8,128)(2,1)S(1)}, u32[]{:S(2)}, u32[]{:S(2)}) %collective-permute-start.5) | collective-permute-done | bytes 655392 | tf_op jit(solution)/shard_map/ppermute | solution.py:279
  71.4 1.2 pad_maximum_fusion.1.ffn_sum
  72.6 12.8 %ffn_back.1 = (bf16[1024,640]{1,0:T(8,128)(2,1)}, bf16[1024,640]{1,0:T(8,128)(2,1)S(1)}, bf16[640,1536]{1,0:T(8,128)(2,1)}, f32[8,640]{1,0:T(8,128)S(1)}) custom-call(bf16[1024,640]{1,0:T(8,128)(2,1)S(1)} %copy-done.5, bf16[1024,640]{1,0:T(8,128)(2,1)S(1)} %pad_maximum_fusion.attn_sum, bf16[1024,640]{1,0:T(8,128)(2,1)} %pad_maximum_fusion.1.ffn_sum, ...), custom_call_target="tpu_custom_call" | custom-call | flops 4026531840 | bytes 11410944 | tf_op jit(solution)/shard_map/ffn_back/pallas_call | solution.py:241
  85.6 2.2 %dynamic-slice_bitcast_fusion = bf16[4,80,1536]{2,1,0:T(8,128)(2,1)} fusion(bf16[4,2,80,1536]{3,2,1,0:T(8,128)(2,1)} %bitcast.46, s32[]{:T(128)S(6)} %select_n.90), kind=kLoop, calls=%fused_computation.21 | loop fusion | bytes 1966084 | tf_op jit(solution)/shard_map/jit(dynamic_index_in_dim)/squeeze | solution.py:305
  87.9 1.7 collective-permute-start.17
  89.7 1.6 collective-permute-start.7
  91.4 15.2 %collective-permute-done.7 = bf16[512,640]{1,0:T(8,128)(2,1)S(1)} collective-permute-done((bf16[512,640]{1,0:T(8,128)(2,1)S(1)}, bf16[512,640]{1,0:T(8,128)(2,1)S(1)}, u32[]{:S(2)}, u32[]{:S(2)}) %collective-permute-start.7) | collective-permute-done | bytes 655392 | tf_op jit(solution)/shard_map/ppermute | solution.py:275
  106.8 5.4 %collective-permute-done.17 = bf16[4,80,1536]{2,1,0:T(8,128)(2,1)} collective-permute-done((bf16[4,80,1536]{2,1,0:T(8,128)(2,1)}, bf16[4,80,1536]{2,1,0:T(8,128)(2,1)}, u32[]{:S(2)}, u32[]{:S(2)}) %collective-permute-start.17) | collective-permute-done | bytes 983072 | tf_op jit(solution)/shard_map/ppermute | solution.py:308
  112.2 1.8 convert_add_fusion.1
  114.0 0.8 fusion.4
  114.8 1.8 collective-permute-start.18
  116.9 1.2 pad_maximum_fusion.2.ffn_back
  118.1 0.6 copy-done.21
  119.8 14.3 %attend_back.1 = (bf16[1024,640]{1,0:T(8,128)(2,1)}, bf16[640,1024]{1,0:T(8,128)(2,1)}, f32[8,640]{1,0:T(8,128)S(1)}, f32[8,256]{1,0:T(8,128)S(1)}) custom-call(bf16[1024,640]{1,0:T(8,128)(2,1)} %tok.7, bf16[1024,640]{1,0:T(8,128)(2,1)} %out_grad.3, bf16[1024,640]{1,0:T(8,128)(2,1)} %pad_maximum_fusion.2.ffn_back, bf16[1024,640]{1,0:T(8,128)(2,1)} %copy-done, ...), custom_call_target="tpu_custom_call" | custom-call | flops 5033164800 | bytes 12856320 | tf_op jit(solution)/shard_map/attend_back/pallas_call | solution.py:241
  134.1 0.5 dynamic-update-slice
  134.6 0.2 dynamic-update-slice.1
  134.8 0.2 dynamic-update-slice.2
  135.0 0.2 dynamic-update-slice.3
  135.2 0.2 dynamic-update-slice.4
  135.7 1.3 fusion.1
  137.0 1.6 collective-permute-start.12
  138.7 1.1 bitcast_add_fusion
  139.9 2.7 %collective-permute-start.19 = (bf16[1,80,1536]{2,1,0:T(8,128)(2,1)S(1)}, bf16[1,80,1536]{2,1,0:T(8,128)(2,1)S(1)}, u32[]{:S(2)}, u32[]{:S(2)}) collective-permute-start(bf16[1,80,1536]{2,1,0:T(8,128)(2,1)S(1)} %dynamic-slice_convert_fusion.2), channel_id=1, source_target_pairs={{0,16},{4,20},{8,24},{12,28},{16,0},{20,4},{24,8},{28,12},{1,17},{... | collective-permute-start | bytes 737288 | tf_op jit(solution)/shard_map/ppermute | solution.py:308
  142.7 1.6 collective-permute-start.10
  144.3 11.4 %collective-permute-done.12 = bf16[4,96,1024]{2,1,0:T(8,128)(2,1)S(1)} collective-permute-done((bf16[4,96,1024]{2,1,0:T(8,128)(2,1)S(1)}, bf16[4,96,1024]{2,1,0:T(8,128)(2,1)S(1)}, u32[]{:S(2)}, u32[]{:S(2)}) %collective-permute-start.12) | collective-permute-done | bytes 786464 | tf_op jit(solution)/shard_map/ppermute | solution.py:308
  155.7 0.3 convert_add_fusion.2
  156.1 0.4 collective-permute-start.13
  156.5 0.8 fusion.6
  157.3 8.2 %collective-permute-done.13 = bf16[2,96,1024]{2,1,0:T(8,128)(2,1)S(1)} collective-permute-done((bf16[2,96,1024]{2,1,0:T(8,128)(2,1)S(1)}, bf16[2,96,1024]{2,1,0:T(8,128)(2,1)S(1)}, u32[]{:S(2)}, u32[]{:S(2)}) %collective-permute-start.13) | collective-permute-done | bytes 393248 | tf_op jit(solution)/shard_map/ppermute | solution.py:308
  165.7 3.5 %collective-permute-start.14 = (bf16[1,96,1024]{2,1,0:T(8,128)(2,1)S(1)}, bf16[1,96,1024]{2,1,0:T(8,128)(2,1)S(1)}, u32[]{:S(2)}, u32[]{:S(2)}) collective-permute-start(bf16[1,96,1024]{2,1,0:T(8,128)(2,1)S(1)} %dynamic-slice_convert_fusion.3), channel_id=1, source_target_pairs={{0,16},{4,20},{8,24},{12,28},{16,0},{20,4},{24,8},{28,12},{1,17},{... | collective-permute-start | bytes 589832 | tf_op jit(solution)/shard_map/ppermute | solution.py:308
  169.5 5.7 %collective-permute-done.14 = bf16[1,96,1024]{2,1,0:T(8,128)(2,1)S(1)} collective-permute-done((bf16[1,96,1024]{2,1,0:T(8,128)(2,1)S(1)}, bf16[1,96,1024]{2,1,0:T(8,128)(2,1)S(1)}, u32[]{:S(2)}, u32[]{:S(2)}) %collective-permute-start.14) | collective-permute-done | bytes 196640 | tf_op jit(solution)/shard_map/ppermute | solution.py:308
  175.3 0.7 fusion.7
  176.0 0.6 collective-permute-done.15
  176.7 1.6 collective-permute-start.16
  178.3 0.6 fusion.11
  178.9 3.1 %collective-permute-done.16 = bf16[112,512]{1,0:T(8,128)(2,1)S(1)} collective-permute-done((bf16[112,512]{1,0:T(8,128)(2,1)S(1)}, bf16[112,512]{1,0:T(8,128)(2,1)S(1)}, u32[]{:S(2)}, u32[]{:S(2)}) %collective-permute-start.16) | collective-permute-done | bytes 114720 | tf_op jit(solution)/shard_map/ppermute | solution.py:290
  182.0 0.6 fusion.10
  182.6 0.6 fusion.9
  183.2 0.7 fusion.8
  184.0 0.9 copy-done.29
  184.9 0.4 copy-done.33
  185.4 1.9 %convert_add_fusion = f32[1024,640]{1,0:T(8,128)} fusion(bf16[1024,640]{1,0:T(8,128)(2,1)S(1)} %copy-done.33, bf16[512,640]{1,0:T(8,128)(2,1)S(1)} %get-tuple-element.60, bf16[512,640]{1,0:T(8,128)(2,1)S(1)} %get-tuple-element.59, bf16[512,640]{1,0:T(8,128)(2,1)S(1)} %copy-done.29, bf16[512,640]{1,0:T(8,128)(2,1)S(1)} %get-tuple-element.61), kind=kLoop, calls=%fused_computation.1 | loop fusion | flops 7208960 | bytes 6553600 | tf_op jit(solution)/shard_map/add | solution.py:392
  (130 shorter events, 4.9 us)
Async XLA Ops:
  0.6 1.8 copy-start.34
  2.0 2.3 %copy-start.9 = (bf16[640,256]{1,0:T(8,128)(2,1)S(1)}, bf16[640,256]{1,0:T(8,128)(2,1)}, u32[]{:S(2)}) copy-start(bf16[640,256]{1,0:T(8,128)(2,1)} %q_w.3) | copy-start | bytes 983044
  2.0 2.3 %copy-start.10 = (bf16[640,256]{1,0:T(8,128)(2,1)S(1)}, bf16[640,256]{1,0:T(8,128)(2,1)}, u32[]{:S(2)}) copy-start(bf16[640,256]{1,0:T(8,128)(2,1)} %k_w.3) | copy-start | bytes 983044
  2.0 2.3 %copy-start.12 = (bf16[640,256]{1,0:T(8,128)(2,1)S(1)}, bf16[640,256]{1,0:T(8,128)(2,1)}, u32[]{:S(2)}) copy-start(bf16[640,256]{1,0:T(8,128)(2,1)} %v_w.3) | copy-start | bytes 983044
  2.1 2.3 %copy-start.14 = (bf16[640,256]{1,0:T(8,128)(2,1)S(1)}, bf16[640,256]{1,0:T(8,128)(2,1)}, u32[]{:S(2)}) copy-start(bf16[640,256]{1,0:T(8,128)(2,1)} %o_w.3) | copy-start | bytes 983044
  2.1 2.3 %copy-start.16 = (f32[256]{0:T(256)S(1)}, f32[256]{0:T(256)}, u32[]{:S(2)}) copy-start(f32[256]{0:T(256)} %param.22) | copy-start | bytes 3076
  2.1 2.3 %copy-start.17 = (f32[256]{0:T(256)S(1)}, f32[256]{0:T(256)}, u32[]{:S(2)}) copy-start(f32[256]{0:T(256)} %param.23) | copy-start | bytes 3076
  4.3 9.0 %copy-start.1 = (f32[1024,128]{1,0:T(8,128)}, f32[1024,128]{1,0:T(8,128)S(1)}, u32[]{:S(2)}) copy-start(f32[1024,128]{1,0:T(8,128)S(1)} %get-tuple-element.80.sin_b.sine_tab) | copy-start | bytes 1572868
  4.3 9.0 %copy-start.3 = (f32[1024,128]{1,0:T(8,128)}, f32[1024,128]{1,0:T(8,128)S(1)}, u32[]{:S(2)}) copy-start(f32[1024,128]{1,0:T(8,128)S(1)} %get-tuple-element.81.cos_b.cosine) | copy-start | bytes 1572868
  13.3 0.9 copy-start.18
  14.2 0.8 copy-start.24
  15.0 0.8 copy-start.26
  15.8 6.3 %copy-start.20 = (bf16[1536,256]{1,0:T(8,128)(2,1)}, bf16[1536,256]{1,0:T(8,128)(2,1)S(1)}, u32[]{:S(2)}) copy-start(bf16[1536,256]{1,0:T(8,128)(2,1)S(1)} %get-tuple-element.46.v_pad) | copy-start | bytes 2359300
  15.8 6.3 %copy-start.22 = (bf16[1024,256]{1,0:T(8,128)(2,1)}, bf16[1024,256]{1,0:T(8,128)(2,1)S(1)}, u32[]{:S(2)}) copy-start(bf16[1024,256]{1,0:T(8,128)(2,1)S(1)} %get-tuple-element.40.attn) | copy-start | bytes 1572868
  15.9 5.1 %copy-start.32 = (bf16[1024,640]{1,0:T(8,128)(2,1)S(1)}, bf16[1024,640]{1,0:T(8,128)(2,1)}, u32[]{:S(2)}) copy-start(bf16[1024,640]{1,0:T(8,128)(2,1)} %get-tuple-element.34) | copy-start | bytes 3932164
  18.3 2.6 %collective-permute-start = (bf16[512,640]{1,0:T(8,128)(2,1)}, bf16[512,640]{1,0:T(8,128)(2,1)}, u32[]{:S(2)}, u32[]{:S(2)}) collective-permute-start(bf16[512,640]{1,0:T(8,128)(2,1)} %constant_dynamic-slice_fusion.3), channel_id=1, source_target_pairs={{0,1},{1,0},{2,3},{3,2},{4,5},{5,4},{6,7},{7,6},{8,9},{9,8},{10,11... | collective-permute-start | bytes 1966088 | tf_op jit(solution)/shard_map/ppermute | solution.py:270
  22.2 18.3 %copy-start.35 = (f32[640]{0:T(1024)S(1)}, f32[640]{0:T(1024)}, u32[]{:S(2)}) copy-start(f32[640]{0:T(1024)} %param.25) | copy-start | bytes 7684
  22.2 18.3 %copy-start.36 = (f32[640]{0:T(1024)S(1)}, f32[640]{0:T(1024)}, u32[]{:S(2)}) copy-start(f32[640]{0:T(1024)} %param.26) | copy-start | bytes 7684
  22.2 18.0 %collective-permute-start.1 = (bf16[512,640]{1,0:T(8,128)(2,1)S(1)}, bf16[512,640]{1,0:T(8,128)(2,1)S(1)}, u32[]{:S(2)}, u32[]{:S(2)}) collective-permute-start(bf16[512,640]{1,0:T(8,128)(2,1)S(1)} %add_convert_fusion.7), channel_id=1, source_target_pairs={{0,2},{1,3},{2,0},{3,1},{4,6},{5,7},{6,4},{7,5},{8,10},{9,11},{10,... | collective-permute-start | bytes 1966088 | tf_op jit(solution)/shard_map/ppermute | solution.py:275
  40.4 2.2 %collective-permute-start.2 = (bf16[512,640]{1,0:T(8,128)(2,1)S(1)}, bf16[512,640]{1,0:T(8,128)(2,1)S(1)}, u32[]{:S(2)}, u32[]{:S(2)}) collective-permute-start(bf16[512,640]{1,0:T(8,128)(2,1)S(1)} %add_convert_fusion.6), channel_id=1, source_target_pairs={{0,1},{1,0},{2,3},{3,2},{4,5},{5,4},{6,7},{7,6},{8,9},{9,8},{10,11... | collective-permute-start | bytes 1966088 | tf_op jit(solution)/shard_map/ppermute | solution.py:279
  42.5 1.1 copy-start.8
  42.7 1.4 copy-start.5
  42.7 1.6 copy-start.6
  42.7 1.8 copy-start.7
  44.5 28.1 %copy-start = (bf16[1024,640]{1,0:T(8,128)(2,1)}, bf16[1024,640]{1,0:T(8,128)(2,1)S(1)}, u32[]{:S(2)}) copy-start(bf16[1024,640]{1,0:T(8,128)(2,1)S(1)} %pad_maximum_fusion.attn_sum) | copy-start | bytes 3932164
  49.7 2.2 %collective-permute-start.3 = (bf16[512,640]{1,0:T(8,128)(2,1)S(1)}, bf16[512,640]{1,0:T(8,128)(2,1)S(1)}, u32[]{:S(2)}, u32[]{:S(2)}) collective-permute-start(bf16[512,640]{1,0:T(8,128)(2,1)S(1)} %constant_dynamic-slice_fusion.2), channel_id=1, source_target_pairs={{0,1},{1,0},{2,3},{3,2},{4,5},{5,4},{6,7},{7,6},{8,9},{9,8},{10,11... | collective-permute-start | bytes 1966088 | tf_op jit(solution)/shard_map/ppermute | solution.py:270
  52.1 17.1 %copy-start.37 = (f32[640]{0:T(1024)S(1)}, f32[640]{0:T(1024)}, u32[]{:S(2)}) copy-start(f32[640]{0:T(1024)} %param.30) | copy-start | bytes 7684
  52.1 16.9 %collective-permute-start.4 = (bf16[512,640]{1,0:T(8,128)(2,1)S(1)}, bf16[512,640]{1,0:T(8,128)(2,1)S(1)}, u32[]{:S(2)}, u32[]{:S(2)}) collective-permute-start(bf16[512,640]{1,0:T(8,128)(2,1)S(1)} %add_convert_fusion.5), channel_id=1, source_target_pairs={{0,2},{1,3},{2,0},{3,1},{4,6},{5,7},{6,4},{7,5},{8,10},{9,11},{10,... | collective-permute-start | bytes 1966088 | tf_op jit(solution)/shard_map/ppermute | solution.py:275
  69.1 2.2 %collective-permute-start.5 = (bf16[512,640]{1,0:T(8,128)(2,1)S(1)}, bf16[512,640]{1,0:T(8,128)(2,1)S(1)}, u32[]{:S(2)}, u32[]{:S(2)}) collective-permute-start(bf16[512,640]{1,0:T(8,128)(2,1)S(1)} %add_convert_fusion.4), channel_id=1, source_target_pairs={{0,1},{1,0},{2,3},{3,2},{4,5},{5,4},{6,7},{7,6},{8,9},{9,8},{10,11... | collective-permute-start | bytes 1966088 | tf_op jit(solution)/shard_map/ppermute | solution.py:279
  85.5 4.1 %collective-permute-start.6 = (bf16[512,640]{1,0:T(8,128)(2,1)S(1)}, bf16[512,640]{1,0:T(8,128)(2,1)S(1)}, u32[]{:S(2)}, u32[]{:S(2)}) collective-permute-start(bf16[512,640]{1,0:T(8,128)(2,1)S(1)} %constant_dynamic-slice_fusion.1), channel_id=1, source_target_pairs={{0,1},{1,0},{2,3},{3,2},{4,5},{5,4},{6,7},{7,6},{8,9},{9,8},{10,11... | collective-permute-start | bytes 1966088 | tf_op jit(solution)/shard_map/ppermute | solution.py:270
  87.9 24.4 %collective-permute-start.17 = (bf16[4,80,1536]{2,1,0:T(8,128)(2,1)}, bf16[4,80,1536]{2,1,0:T(8,128)(2,1)}, u32[]{:S(2)}, u32[]{:S(2)}) collective-permute-start(bf16[4,80,1536]{2,1,0:T(8,128)(2,1)} %dynamic-slice_bitcast_fusion), channel_id=1, source_target_pairs={{0,4},{4,0},{8,12},{12,8},{16,20},{20,16},{24,28},{28,24},{1,5},{5... | collective-permute-start | bytes 2949128 | tf_op jit(solution)/shard_map/ppermute | solution.py:308
  89.7 16.8 %collective-permute-start.7 = (bf16[512,640]{1,0:T(8,128)(2,1)S(1)}, bf16[512,640]{1,0:T(8,128)(2,1)S(1)}, u32[]{:S(2)}, u32[]{:S(2)}) collective-permute-start(bf16[512,640]{1,0:T(8,128)(2,1)S(1)} %add_convert_fusion.3), channel_id=1, source_target_pairs={{0,2},{1,3},{2,0},{3,1},{4,6},{5,7},{6,4},{7,5},{8,10},{9,11},{10,... | collective-permute-start | bytes 1966088 | tf_op jit(solution)/shard_map/ppermute | solution.py:275
  106.7 9.9 %collective-permute-start.8 = (bf16[512,640]{1,0:T(8,128)(2,1)S(1)}, bf16[512,640]{1,0:T(8,128)(2,1)S(1)}, u32[]{:S(2)}, u32[]{:S(2)}) collective-permute-start(bf16[512,640]{1,0:T(8,128)(2,1)S(1)} %add_convert_fusion.2), channel_id=1, source_target_pairs={{0,1},{1,0},{2,3},{3,2},{4,5},{5,4},{6,7},{7,6},{8,9},{9,8},{10,11... | collective-permute-start | bytes 1966088 | tf_op jit(solution)/shard_map/ppermute | solution.py:279
  114.8 23.8 %collective-permute-start.18 = (bf16[2,80,1536]{2,1,0:T(8,128)(2,1)}, bf16[2,80,1536]{2,1,0:T(8,128)(2,1)}, u32[]{:S(2)}, u32[]{:S(2)}) collective-permute-start(bf16[2,80,1536]{2,1,0:T(8,128)(2,1)} %fusion.4), channel_id=1, source_target_pairs={{0,8},{4,12},{8,0},{12,4},{16,24},{20,28},{24,16},{28,20},{1,9},{5... | collective-permute-start | bytes 1474568 | tf_op jit(solution)/shard_map/ppermute | solution.py:308
  116.6 1.4 copy-start.19
  116.6 2.1 %copy-start.21 = (bf16[1536,256]{1,0:T(8,128)(2,1)S(1)}, bf16[1536,256]{1,0:T(8,128)(2,1)}, u32[]{:S(2)}) copy-start(bf16[1536,256]{1,0:T(8,128)(2,1)} %copy-done.20) | copy-start | bytes 2359300
  116.6 2.2 %copy-start.25 = (bf16[1024,256]{1,0:T(8,128)(2,1)S(1)}, bf16[1024,256]{1,0:T(8,128)(2,1)}, u32[]{:S(2)}) copy-start(bf16[1024,256]{1,0:T(8,128)(2,1)} %copy-done.24) | copy-start | bytes 1572868
  116.6 2.4 %copy-start.27 = (f32[1024,128]{1,0:T(8,128)S(1)}, f32[1024,128]{1,0:T(8,128)}, u32[]{:S(2)}) copy-start(f32[1024,128]{1,0:T(8,128)} %copy-done.26) | copy-start | bytes 1572868
  116.8 1.3 copy-start.28
  116.8 2.4 %copy-start.2 = (f32[1024,128]{1,0:T(8,128)S(1)}, f32[1024,128]{1,0:T(8,128)}, u32[]{:S(2)}) copy-start(f32[1024,128]{1,0:T(8,128)} %copy-done.1) | copy-start | bytes 1572868
  116.8 2.5 %copy-start.4 = (f32[1024,128]{1,0:T(8,128)S(1)}, f32[1024,128]{1,0:T(8,128)}, u32[]{:S(2)}) copy-start(f32[1024,128]{1,0:T(8,128)} %copy-done.3) | copy-start | bytes 1572868
  116.8 2.6 %copy-start.11 = (bf16[640,256]{1,0:T(8,128)(2,1)S(1)}, bf16[640,256]{1,0:T(8,128)(2,1)}, u32[]{:S(2)}) copy-start(bf16[640,256]{1,0:T(8,128)(2,1)} %k_w.3) | copy-start | bytes 983044
  116.8 2.7 %copy-start.13 = (bf16[640,256]{1,0:T(8,128)(2,1)S(1)}, bf16[640,256]{1,0:T(8,128)(2,1)}, u32[]{:S(2)}) copy-start(bf16[640,256]{1,0:T(8,128)(2,1)} %v_w.3) | copy-start | bytes 983044
  116.8 2.8 %copy-start.15 = (bf16[640,256]{1,0:T(8,128)(2,1)S(1)}, bf16[640,256]{1,0:T(8,128)(2,1)}, u32[]{:S(2)}) copy-start(bf16[640,256]{1,0:T(8,128)(2,1)} %o_w.3) | copy-start | bytes 983044
  116.8 2.9 %copy-start.23 = (bf16[1024,256]{1,0:T(8,128)(2,1)S(1)}, bf16[1024,256]{1,0:T(8,128)(2,1)}, u32[]{:S(2)}) copy-start(bf16[1024,256]{1,0:T(8,128)(2,1)} %copy-done.22) | copy-start | bytes 1572868
  135.7 2.9 %copy-start.31 = (bf16[1024,640]{1,0:T(8,128)(2,1)S(1)}, bf16[1024,640]{1,0:T(8,128)(2,1)}, u32[]{:S(2)}) copy-start(bf16[1024,640]{1,0:T(8,128)(2,1)} %get-tuple-element.47) | copy-start | bytes 3932164
  137.0 18.7 %collective-permute-start.12 = (bf16[4,96,1024]{2,1,0:T(8,128)(2,1)S(1)}, bf16[4,96,1024]{2,1,0:T(8,128)(2,1)S(1)}, u32[]{:S(2)}, u32[]{:S(2)}) collective-permute-start(bf16[4,96,1024]{2,1,0:T(8,128)(2,1)S(1)} %fusion.1), channel_id=1, source_target_pairs={{0,4},{4,0},{8,12},{12,8},{16,20},{20,16},{24,28},{28,24},{1,5},{5... | collective-permute-start | bytes 2359304 | tf_op jit(solution)/shard_map/ppermute | solution.py:308
  138.6 3.9 %collective-permute-start.9 = (bf16[512,640]{1,0:T(8,128)(2,1)S(1)}, bf16[512,640]{1,0:T(8,128)(2,1)S(1)}, u32[]{:S(2)}, u32[]{:S(2)}) collective-permute-start(bf16[512,640]{1,0:T(8,128)(2,1)S(1)} %constant_dynamic-slice_fusion), channel_id=1, source_target_pairs={{0,1},{1,0},{2,3},{3,2},{4,5},{5,4},{6,7},{7,6},{8,9},{9,8},{10,11... | collective-permute-start | bytes 1966088 | tf_op jit(solution)/shard_map/ppermute | solution.py:270
  139.8 15.9 %copy-start.30 = (bf16[640,1024]{1,0:T(8,128)(2,1)S(1)}, bf16[640,1024]{1,0:T(8,128)(2,1)}, u32[]{:S(2)}) copy-start(bf16[640,1024]{1,0:T(8,128)(2,1)} %get-tuple-element.48) | copy-start | bytes 3932164
  139.9 16.6 %collective-permute-start.19 = (bf16[1,80,1536]{2,1,0:T(8,128)(2,1)S(1)}, bf16[1,80,1536]{2,1,0:T(8,128)(2,1)S(1)}, u32[]{:S(2)}, u32[]{:S(2)}) collective-permute-start(bf16[1,80,1536]{2,1,0:T(8,128)(2,1)S(1)} %dynamic-slice_convert_fusion.2), channel_id=1, source_target_pairs={{0,16},{4,20},{8,24},{12,28},{16,0},{20,4},{24,8},{28,12},{1,17},{... | collective-permute-start | bytes 737288 | tf_op jit(solution)/shard_map/ppermute | solution.py:308
  142.7 26.5 %collective-permute-start.10 = (bf16[512,640]{1,0:T(8,128)(2,1)S(1)}, bf16[512,640]{1,0:T(8,128)(2,1)S(1)}, u32[]{:S(2)}, u32[]{:S(2)}) collective-permute-start(bf16[512,640]{1,0:T(8,128)(2,1)S(1)} %add_convert_fusion.1), channel_id=1, source_target_pairs={{0,2},{1,3},{2,0},{3,1},{4,6},{5,7},{6,4},{7,5},{8,10},{9,11},{10,... | collective-permute-start | bytes 1966088 | tf_op jit(solution)/shard_map/ppermute | solution.py:275
  156.1 9.5 %collective-permute-start.13 = (bf16[2,96,1024]{2,1,0:T(8,128)(2,1)S(1)}, bf16[2,96,1024]{2,1,0:T(8,128)(2,1)S(1)}, u32[]{:S(2)}, u32[]{:S(2)}) collective-permute-start(bf16[2,96,1024]{2,1,0:T(8,128)(2,1)S(1)} %fusion.5), channel_id=1, source_target_pairs={{0,8},{4,12},{8,0},{12,4},{16,24},{20,28},{24,16},{28,20},{1,9},{5... | collective-permute-start | bytes 1179656 | tf_op jit(solution)/shard_map/ppermute | solution.py:308
  165.7 9.4 %collective-permute-start.14 = (bf16[1,96,1024]{2,1,0:T(8,128)(2,1)S(1)}, bf16[1,96,1024]{2,1,0:T(8,128)(2,1)S(1)}, u32[]{:S(2)}, u32[]{:S(2)}) collective-permute-start(bf16[1,96,1024]{2,1,0:T(8,128)(2,1)S(1)} %dynamic-slice_convert_fusion.3), channel_id=1, source_target_pairs={{0,16},{4,20},{8,24},{12,28},{16,0},{20,4},{24,8},{28,12},{1,17},{... | collective-permute-start | bytes 589832 | tf_op jit(solution)/shard_map/ppermute | solution.py:308
  169.4 14.5 %collective-permute-start.11 = (bf16[512,640]{1,0:T(8,128)(2,1)S(1)}, bf16[512,640]{1,0:T(8,128)(2,1)S(1)}, u32[]{:S(2)}, u32[]{:S(2)}) collective-permute-start(bf16[512,640]{1,0:T(8,128)(2,1)S(1)} %add_convert_fusion), channel_id=1, source_target_pairs={{0,1},{1,0},{2,3},{3,2},{4,5},{5,4},{6,7},{7,6},{8,9},{9,8},{10,11... | collective-permute-start | bytes 1966088 | tf_op jit(solution)/shard_map/ppermute | solution.py:279
  175.2 1.4 collective-permute-start.15
  176.7 5.3 %collective-permute-start.16 = (bf16[112,512]{1,0:T(8,128)(2,1)S(1)}, bf16[112,512]{1,0:T(8,128)(2,1)S(1)}, u32[]{:S(2)}, u32[]{:S(2)}) collective-permute-start(bf16[112,512]{1,0:T(8,128)(2,1)S(1)} %add_convert_fusion.8), channel_id=1, source_target_pairs={{0,2},{1,3},{2,0},{3,1},{4,6},{5,7},{6,4},{7,5},{8,10},{9,11},{10,... | collective-permute-start | bytes 344072 | tf_op jit(solution)/shard_map/ppermute | solution.py:290
  183.9 1.1 copy-start.29
  183.9 1.5 copy-start.33
where the time goes:
time: 188 us; the launch traced here: 187 us
  waiting for transfers between devices  87.8 us (47%)
  Pallas kernels  41.2 us (22%)
  starting transfers between devices  22.5 us (12%)
  local copies, waits for them, and re-layouts  19.1 us (10%)
  other arithmetic  15.3 us (8%)
    ppermute x4, waiting for transfers between devices, sum_tensor(): got = lax.ppermute(sent, 'tensor', flip_pairs(size, bit))  45.2 us
    pallas_call x4, Pallas kernels, row_call(): pl.pallas_call(kernel, name=name, out_shape=tuple((jax.ShapeDtypeStruct(s...  41.2 us
    ppermute x6, waiting for transfers between devices, scatter_dp(): got = lax.ppermute(sent, 'dp', flip_pairs(size, bit))  30.8 us
    ppermute x6, starting transfers between devices, scatter_dp(): got = lax.ppermute(sent, 'dp', flip_pairs(size, bit))  11.6 us
    unnamed x83, local copies, waits for them, and re-layouts  8.74 us
    ppermute x4, starting transfers between devices, sum_tensor(): got = lax.ppermute(sent, 'tensor', flip_pairs(size, bit))  7.95 us
    ppermute x4, waiting for transfers between devices, sum_tensor(): got = lax.ppermute(sent, 'tensor', flip_pairs(size, 1))  4.1 us
    ppermute x4, waiting for transfers between devices, sum_tensor(): got = lax.ppermute(other, 'tensor', flip_pairs(size, 1))  4.03 us
  transfers between devices with their start and end apart: 20, of which 13 were waited for; matrix products, arithmetic and copies ran while one was open for 8% of the time, Pallas kernels for 8%

commit v1 on v0

--- a/solution.py
+++ b/solution.py
@@ -260,37 +260,171 @@
     return [(index, index ^ bit) for index in range(size)]
 
 
-def sum_tensor(term, size):
-    rows = term.shape[0]
-    half = rows // 2
-    low = lax.rem(lax.axis_index("tensor"), 2)
-    term = lax.optimization_barrier(term.astype(jnp.bfloat16))
-    mine = lax.dynamic_slice_in_dim(term, low * half, half, 0)
-    other = lax.dynamic_slice_in_dim(term, (1 - low) * half, half, 0)
-    got = lax.ppermute(other, "tensor", flip_pairs(size, 1))
-    total = mine.astype(jnp.float32) + got.astype(jnp.float32)
-    bit = 2
-    while bit < size:
-        sent = lax.optimization_barrier(total.astype(jnp.bfloat16))
-        got = lax.ppermute(sent, "tensor", flip_pairs(size, bit))
-        total = sent.astype(jnp.float32) + got.astype(jnp.float32)
-        bit *= 2
-    sent = lax.optimization_barrier(total.astype(jnp.bfloat16))
-    got = lax.ppermute(sent, "tensor", flip_pairs(size, 1))
-    first = jnp.where(low == 0, sent, got)
-    second = jnp.where(low == 0, got, sent)
-    return jnp.concatenate([first, second], axis=0)
-
-
-def sum_small(values, size):
-    total = values
-    bit = 1
-    while bit < size:
-        sent = lax.optimization_barrier(total.astype(jnp.bfloat16))
-        got = lax.ppermute(sent, "tensor", flip_pairs(size, bit))
-        total = sent.astype(jnp.float32) + got.astype(jnp.float32)
-        bit *= 2
-    return total
+def flip(index, bit):
+    return index + bit - 2 * bit * (lax.div(index, bit) % 2)
+
+
+def send(src, dst, sems, slot, device):
+    copy = pltpu.make_async_remote_copy(
+        src_ref=src,
+        dst_ref=dst,
+        send_sem=sems.at[0, slot],
+        recv_sem=sems.at[1, slot],
+        device_id=device,
+        device_id_type=pl.DeviceIdType.MESH,
+    )
+    copy.start()
+    return copy
+
+
+def exchange_kernel(chunks, orders, *refs):
+    count = len(orders)
+    term, blocks, refs = refs[0], refs[1 : 1 + count], refs[1 + count :]
+    total, reduced, refs = refs[0], refs[1 : 1 + count], refs[1 + count :]
+    core_got, y_sent, y_got, back_got, sems = refs[:5]
+    scatter_refs = refs[5:]
+    me = lax.axis_index("tensor")
+    low = me % 2
+    core_peer, y_peer = flip(me, 1), flip(me, 2)
+    diagonal = flip(y_peer, 1)
+    barrier = pltpu.get_barrier_semaphore()
+    greeted = [{"tensor": core_peer}, {"tensor": y_peer}]
+    if count:
+        spot = lax.axis_index("dp")
+        greeted.append({"tensor": diagonal})
+        greeted += [{"dp": flip(spot, bit)} for bit in sorted(orders[0])]
+    for device in greeted:
+        pl.semaphore_signal(
+            barrier, inc=1, device_id=device, device_id_type=pl.DeviceIdType.MESH
+        )
+    pl.semaphore_wait(barrier, len(greeted))
+
+    half = term.shape[0] // 2
+    size = half // chunks
+
+    def rows(side, chunk):
+        return pl.ds(pl.multiple_of(side * half + chunk * size, size), size)
+
+    copies = []
+    first = [
+        send(term.at[rows(1 - low, c)], core_got.at[c], sems, c, {"tensor": core_peer})
+        for c in range(chunks)
+    ]
+    copies += first
+
+    state = []
+    if count:
+        scatter_sems = scatter_refs[-1]
+        depth = len(orders[0])
+        slot = 0
+        for g, order in enumerate(orders):
+            own = scatter_refs[g * 2 * depth : (g + 1) * 2 * depth]
+            state.append({"order": order, "got": own[:depth], "kept": own[depth:], "src": blocks[g]})
+
+        def start_stage(g, stage):
+            entry = state[g]
+            bit = entry["order"][stage]
+            mine = lax.div(spot, bit) % 2
+            width = entry["src"].shape[0] // 2
+            entry["copy"] = send(
+                entry["src"].at[pl.ds((1 - mine) * width, width)],
+                entry["got"][stage],
+                scatter_sems,
+                g * depth + stage,
+                {"dp": flip(spot, bit)},
+            )
+            copies.append(entry["copy"])
+
+        def finish_stage(g, stage):
+            entry = state[g]
+            mine = lax.div(spot, entry["order"][stage]) % 2
+            width = entry["src"].shape[0] // 2
+            entry["copy"].wait_recv()
+            for item in range(width):
+                added = entry["src"][mine * width + item].astype(F32)
+                added = added + entry["got"][stage][item].astype(F32)
+                if stage == depth - 1:
+                    reduced[g][...] = added
+                entry["kept"][stage][item] = added.astype(BF16)
+            entry["src"] = entry["kept"][stage]
+
+        for g in range(count):
+            start_stage(g, 0)
+
+    second = []
+    for c in range(chunks):
+        first[c].wait_recv()
+        y_sent[c] = (term[rows(low, c), :].astype(F32) + core_got[c].astype(F32)).astype(BF16)
+        second.append(send(y_sent.at[c], y_got.at[c], sems, chunks + c, {"tensor": y_peer}))
+    copies += second
+    if count:
+        for g in range(count):
+            finish_stage(g, 0)
+            if depth > 1:
+                start_stage(g, 1)
+    third = []
+    for c in range(chunks):
+        second[c].wait_recv()
+        mine = rows(low, c)
+        total[mine, :] = (y_sent[c].astype(F32) + y_got[c].astype(F32)).astype(BF16)
+        third.append(send(total.at[mine], back_got.at[c], sems, 2 * chunks + c, {"tensor": core_peer}))
+    copies += third
+    for stage in range(1, depth if count else 1):
+        for g in range(count):
+            finish_stage(g, stage)
+            if stage + 1 < depth:
+                start_stage(g, stage + 1)
+    if count:
+        shared, shared_got = state[-1]["kept"][-1], scatter_refs[-2]
+        final = [
+            send(shared.at[0], shared_got.at[d], scatter_sems, count * depth + d, {"tensor": peer})
+            for d, peer in enumerate((core_peer, y_peer, diagonal))
+        ]
+        copies += final
+    for c in range(chunks):
+        third[c].wait_recv()
+        total[rows(1 - low, c), :] = back_got[c]
+    if count:
+        for copy in final:
+            copy.wait_recv()
+        pair = shared[0].astype(F32) + shared_got[0].astype(F32)
+        reduced[-1][...] = pair + (shared_got[1].astype(F32) + shared_got[2].astype(F32))
+    for copy in copies:
+        copy.wait_send()
+
+
+def sum_tensor(term, tensor_size, collective, blocks=(), orders=()):
+    assert tensor_size == 4
+    tok_count, model = term.shape
+    chunks = 4
+    size = tok_count // 2 // chunks
+    buffers = [pltpu.VMEM((chunks, size, model), BF16)] * 4
+    scratch = buffers + [pltpu.SemaphoreType.DMA((2, 3 * chunks))]
+    outs = [jax.ShapeDtypeStruct(term.shape, BF16)]
+    if blocks:
+        depth = len(orders[0])
+        for part in blocks:
+            block = part.shape[1:]
+            widths = [part.shape[0] >> (stage + 1) for stage in range(depth)]
+            scratch += [pltpu.VMEM((width,) + block, BF16) for width in widths] * 2
+            outs.append(jax.ShapeDtypeStruct(block, F32))
+        scratch.append(pltpu.VMEM((3,) + blocks[-1].shape[1:], BF16))
+        scratch.append(pltpu.SemaphoreType.DMA((2, len(blocks) * depth + 3)))
+    result = pl.pallas_call(
+        functools.partial(exchange_kernel, chunks, orders),
+        name="exchange%d" % collective,
+        out_shape=tuple(outs),
+        in_specs=[pl.BlockSpec(memory_space=pltpu.VMEM)] * (1 + len(blocks)),
+        out_specs=tuple(pl.BlockSpec(memory_space=pltpu.VMEM) for _ in outs),
+        scratch_shapes=scratch,
+        compiler_params=pltpu.CompilerParams(
+            collective_id=collective, has_side_effects=True, vmem_limit_bytes=40 * 1024 * 1024
+        ),
+        cost_estimate=pl.CostEstimate(
+            flops=16 * tok_count * model * 640, bytes_accessed=4 * term.size, transcendentals=0
+        ),
+    )(term, *blocks)
+    return result if blocks else result[0]
 
 
 def scatter_dp(blocks, size):
@@ -363,14 +497,14 @@
         ((wide, BF16), (heads, BF16), (heads, BF16), ((tok_count, 128), F32), (heads, F32), (heads, F32)),
         ((padded, BF16), (padded, BF16)), (), 14 * square, False,
     )
-    attn_sum = sum_tensor(term, tensor_size)
+    attn_sum = sum_tensor(term, tensor_size, 0)
     hidden_shape = (tok_count, units)
     term, gate, up = row_call(
         ffn_kernel, "ffn", steps, (tokens, attn_sum),
         (pa_gain, pre_gain, gate_weight, up_weight, down_weight),
         ((wide, BF16), (hidden_shape, F32), (hidden_shape, F32)), (), (), 12 * square, False,
     )
-    ffn_sum = sum_tensor(term, tensor_size)
+    ffn_sum = sum_tensor(term, tensor_size, 1)
     output, term, early, ffn_gains = row_call(
         ffn_back_kernel, "ffn_back", steps, (tokens, attn_sum, ffn_sum, out_grad, gate, up),
         (pa_gain, pre_gain, pf_gain, gate_weight, up_weight, down_weight),
@@ -379,7 +513,7 @@
     )
     part_rows = model // dp_size
     early = scatter_dp(early.reshape(dp_size, part_rows, 3 * units), dp_size)
-    ffn_back = sum_tensor(term, tensor_size)
+    ffn_back = sum_tensor(term, tensor_size, 2)
     term, late, attn_gains, head_gains = row_call(
         attend_back_kernel, "attend_back", steps,
         (tokens, out_grad, ffn_back, attn_sum, attn, q_rot, stats, q_unit, k_unit, cosine, sine_tab, low),
@@ -388,30 +522,44 @@
         (pltpu.VMEM((model, 4 * head_dim), F32), pltpu.VMEM(padded, F32), pltpu.VMEM(padded, F32)),
         30 * square, True,
     )
-    attn_back = sum_tensor(term, tensor_size)
+    gains = jnp.concatenate(
+        [
+            attn_gains[0] / tensor_size,
+            ffn_gains[0] / tensor_size,
+            attn_gains[1],
+            ffn_gains[1],
+            head_gains[0],
+            head_gains[1],
+        ]
+    )
+    gain_count = gains.shape[0]
+    cols = 2 * head_dim
+    gain_rows = -(-gain_count // (16 * cols)) * 16
+    gains = jnp.pad(gains, (0, gain_rows * cols - gain_count)).reshape(1, gain_rows, cols)
+    gains = jnp.broadcast_to(gains.astype(BF16), (dp_size, gain_rows, cols))
+    late = late.reshape(dp_size, part_rows, 2 * cols)
+    bits = dp_size.bit_length() - 1
+    plain = tuple(1 << k for k in range(bits))
+    orders = (plain, plain[1::-1] + plain[2:])
+
+    def ordered(part, order):
+        shape = (2,) * bits + part.shape[1:]
+        axes = tuple(bits - bit.bit_length() for bit in order) + (bits, bits + 1)
+        return part.reshape(shape).transpose(axes).reshape(part.shape)
+
+    blocks = (
+        ordered(late[:, :, :cols], orders[0]),
+        ordered(jnp.concatenate([late[:, :, cols:], gains], axis=1), orders[1]),
+    )
+    attn_back, first_part, shared = sum_tensor(term, tensor_size, 3, blocks, orders)
     grad_tokens = out_grad.astype(F32) + ffn_back.astype(F32) + attn_back.astype(F32)
-    gains = jnp.concatenate(
-        [attn_gains[0], ffn_gains[0], attn_gains[1], ffn_gains[1], head_gains[0], head_gains[1]]
-    )
-    gain_count = gains.shape[0]
-    late_cols = 4 * head_dim
-    gain_rows = -(-gain_count // (16 * late_cols)) * 16
-    gains = jnp.pad(gains, (0, gain_rows * late_cols - gain_count)).reshape(1, gain_rows, late_cols)
-    gains = jnp.broadcast_to(gains.astype(BF16), (dp_size, gain_rows, late_cols))
-    late = jnp.concatenate([late.reshape(dp_size, part_rows, late_cols), gains], axis=1)
-    late = scatter_dp(late, dp_size)
-    grad_o_w = late[:part_rows, :head_dim]
-    grad_q_w = late[:part_rows, head_dim : 2 * head_dim]
-    gain_part = late[part_rows:].reshape(-1)[:gain_count]
-    shared = jnp.concatenate(
-        [late[:part_rows, 2 * head_dim :], late[part_rows:].reshape(2 * gain_rows, 2 * head_dim)], axis=0
-    )
-    shared = sum_small(shared, tensor_size)
+    grad_o_w = first_part[:, :head_dim]
+    grad_q_w = first_part[:, head_dim:]
     grad_k_w = shared[:part_rows, :head_dim]
     grad_v_w = shared[:part_rows, head_dim:]
     gain_sum = shared[part_rows:].reshape(-1)
-    grad_post_attn = gain_part[:model]
-    grad_post_ffn = gain_part[model : 2 * model]
+    grad_post_attn = gain_sum[:model]
+    grad_post_ffn = gain_sum[model : 2 * model]
     grad_input_gain = gain_sum[2 * model : 3 * model]
     grad_pre_ffn = gain_sum[3 * model : 4 * model]
     grad_query_gain = gain_sum[4 * model : 4 * model + head_dim]

time: 188 us -> 198 us (1.053)
  Pallas kernels: 41.2 us -> 136 us
  waiting for transfers between devices: 87.8 us -> 21 us
  starting transfers between devices: 22.5 us -> 3.57 us
  local copies, waits for them, and re-layouts: 19.1 us -> 26.1 us
  other arithmetic: 15.3 us -> 9.87 us
    pallas_call x0 -> x4, Pallas kernels: none -> 95.4 us  [sum_tensor(): pl.pallas_call(functools.partial(exchange_kernel, chunks, orders), name='...]
    ppermute x14 -> x0, waiting for transfers between devices: 57 us -> none  [the longest x4 45.2 us: sum_tensor(): got = lax.ppermute(sent, 'tensor', flip_pairs(size, bit))]
    ppermute x14 -> x0, starting transfers between devices: 10.9 us -> none  [the longest x4 7.95 us: sum_tensor(): got = lax.ppermute(sent, 'tensor', flip_pairs(size, bit))]
    ppermute x6 -> x3, waiting for transfers between devices: 30.8 us -> 21 us  [scatter_dp(): got = lax.ppermute(sent, 'dp', flip_pairs(size, bit))]
    unnamed x83 -> x87, local copies, waits for them, and re-layouts: 8.74 us -> 18.3 us
    ppermute x6 -> x3, starting transfers between devices: 11.6 us -> 3.57 us  [scatter_dp(): got = lax.ppermute(sent, 'dp', flip_pairs(size, bit))]
    dynamic_slice x4 -> x0, local copies, waits for them, and re-layouts: 2.66 us -> none  [sum_tensor(): other = lax.dynamic_slice_in_dim(term, (1 - low) * half, half, 0)]
    concatenate x4 -> x1, other arithmetic: 2.5 us -> 0.05 us  [on_device(): jnp.concatenate([late[:, :, cols:], gains], axis=1)]
  transfers between devices with their start and end apart: 20 -> 3, of which waited for: 13 -> 2; matrix products, arithmetic and copies ran while one was open for 8% -> 4% of each run, Pallas kernels for 8% -> 35%
where the time goes in v1:
time: 198 us
  Pallas kernels  136 us (69%)
  local copies, waits for them, and re-layouts  26.1 us (13%)
  waiting for transfers between devices  21 us (11%)
  other arithmetic  9.87 us (5%)
  starting transfers between devices  3.57 us (2%)
    pallas_call x4, Pallas kernels, sum_tensor(): pl.pallas_call(functools.partial(exchange_kernel, chunks, orders), name='...  95.4 us
    pallas_call x4, Pallas kernels, row_call(): pl.pallas_call(kernel, name=name, out_shape=tuple((jax.ShapeDtypeStruct(s...  40.7 us
    ppermute x3, waiting for transfers between devices, scatter_dp(): got = lax.ppermute(sent, 'dp', flip_pairs(size, bit))  21 us
    unnamed x87, local copies, waits for them, and re-layouts  18.3 us
  transfers between devices with their start and end apart: 3, of which 2 were waited for; matrix products, arithmetic and copies ran while one was open for 4% of the time, Pallas kernels for 35%

profile of v1, /device:TPU:0, one launch (start us, length us, event | category | flops | bytes accessed | tf_op | source)
XLA Modules:
  0.0 197.8 jit_solution(1768736639608378758)
XLA Ops:
  0.6 0.0 copy-start.16
  0.7 0.0 copy-start.17
  0.7 0.0 copy-start.9
  0.7 0.0 copy-start.10
  0.7 0.0 copy-start.12
  0.7 0.0 copy-start.14
  0.7 1.4 convert_reduce_fusion
  2.1 0.2 copy.35
  2.3 0.1 add_maximum_fusion.low_b.low
  2.4 0.7 broadcast_in_dim.27.gain.in_gain
  3.1 1.9 multiply_sine_fusion
  5.0 8.9 %attend.1 = (bf16[1024,640]{1,0:T(8,128)(2,1)}, bf16[1024,256]{1,0:T(8,128)(2,1)S(1)}, bf16[1024,256]{1,0:T(8,128)(2,1)S(1)}, f32[1024,128]{1,0:T(8,128)S(1)}, f...) custom-call(bf16[1024,640]{1,0:T(8,128)(2,1)} %tok.7, ...), custom_call_target="tpu_custom_call" | custom-call | flops 2348810240 | bytes 3678720 | tf_op jit(solution)/shard_map/attend/pallas_call | solution.py:241
  13.9 1.0 copy-done.25
  14.9 1.0 copy-done.27
  15.8 0.8 copy-done.29
  16.6 0.8 copy-done.31
  17.4 0.8 copy-done.33
  18.2 1.3 copy-done.23
  19.5 0.0 copy-start.5
  19.5 0.0 copy-start.7
  19.6 20.7 %exchange0.1.attn_sum = bf16[1024,640]{1,0:T(8,128)(2,1)S(1)} custom-call(bf16[1024,640]{1,0:T(8,128)(2,1)S(1)} %copy-done.23), custom_call_target="tpu_custom_call" | custom-call | flops 6710886400 | bytes 2621440 | tf_op jit(solution)/shard_map/exchange0/pallas_call | solution.py:413
  40.3 5.3 %ffn.1 = (bf16[1024,640]{1,0:T(8,128)(2,1)S(1)}, f32[1024,512]{1,0:T(8,128)}, f32[1024,512]{1,0:T(8,128)}) custom-call(bf16[1024,640]{1,0:T(8,128)(2,1)S(1)} %copy-done.2, bf16[1024,640]{1,0:T(8,128)(2,1)S(1)} %exchange0.1.attn_sum, f32[1,640]{1,0:T(1,128)S(1)} %broadcast_in_dim.30.pa_gain, f32[1,640]{1,0:T(1,128)S(1)} %broadcast_in_dim.31.pre_gain, ...), custom_call_target="tpu_custom_call" | custom-call | flops 2013265920 | bytes 4592640 | tf_op jit(solution)/shard_map/ffn/pallas_call | solution.py:241
  45.6 19.6 %exchange1.1.ffn_sum = bf16[1024,640]{1,0:T(8,128)(2,1)S(1)} custom-call(bf16[1024,640]{1,0:T(8,128)(2,1)S(1)} %get-tuple-element.38.refs_0_), custom_call_target="tpu_custom_call" | custom-call | flops 6710886400 | bytes 2621440 | tf_op jit(solution)/shard_map/exchange1/pallas_call | solution.py:413
  65.2 1.1 copy-done.22
  66.3 0.0 copy-done.39
  66.4 1.1 copy-done.4
  67.4 1.1 copy-done.6
  68.5 1.1 copy-done.8
  69.6 1.3 copy-done.19
  70.9 12.6 %ffn_back.1 = (bf16[1024,640]{1,0:T(8,128)(2,1)}, bf16[1024,640]{1,0:T(8,128)(2,1)S(1)}, bf16[640,1536]{1,0:T(8,128)(2,1)}, f32[8,640]{1,0:T(8,128)S(1)}) custom-call(bf16[1024,640]{1,0:T(8,128)(2,1)S(1)} %copy-done.2, bf16[1024,640]{1,0:T(8,128)(2,1)S(1)} %copy-done.19, bf16[1024,640]{1,0:T(8,128)(2,1)} %copy-done.22, bf16[1024,640]{1,0:T(8,128)(2,1)} %out_grad.3, ...), custom_call_target="tpu_custom_call" | custom-call | flops 4026531840 | bytes 11410944 | tf_op jit(solution)/shard_map/ffn_back/pallas_call | solution.py:241
  83.6 1.1 copy-done.20
  84.6 2.2 %dynamic-slice_bitcast_fusion = bf16[4,80,1536]{2,1,0:T(8,128)(2,1)} fusion(bf16[4,2,80,1536]{3,2,1,0:T(8,128)(2,1)} %bitcast.41, s32[]{:T(128)S(6)} %select_n.22), kind=kLoop, calls=%fused_computation.5 | loop fusion | bytes 1966084 | tf_op jit(solution)/shard_map/jit(dynamic_index_in_dim)/squeeze | solution.py:439
  86.8 2.0 %collective-permute-start = (bf16[4,80,1536]{2,1,0:T(8,128)(2,1)}, bf16[4,80,1536]{2,1,0:T(8,128)(2,1)}, u32[]{:S(2)}, u32[]{:S(2)}) collective-permute-start(bf16[4,80,1536]{2,1,0:T(8,128)(2,1)} %dynamic-slice_bitcast_fusion), channel_id=1, source_target_pairs={{0,4},{4,0},{8,12},{12,8},{16,20},{20,16},{24,28},{28,24},{1,5},{5... | collective-permute-start | bytes 2949128 | tf_op jit(solution)/shard_map/ppermute | solution.py:442
  88.8 1.3 copy-done.21
  90.2 19.8 %exchange2.1.ffn_back = bf16[1024,640]{1,0:T(8,128)(2,1)S(1)} custom-call(bf16[1024,640]{1,0:T(8,128)(2,1)S(1)} %copy-done.21), custom_call_target="tpu_custom_call" | custom-call | flops 6710886400 | bytes 2621440 | tf_op jit(solution)/shard_map/exchange2/pallas_call | solution.py:413
  110.0 0.0 copy-start
  110.0 1.0 copy-done
  111.1 13.9 %attend_back.1 = (bf16[1024,640]{1,0:T(8,128)(2,1)}, bf16[640,1024]{1,0:T(8,128)(2,1)}, f32[8,640]{1,0:T(8,128)S(1)}, f32[8,256]{1,0:T(8,128)S(1)}) custom-call(bf16[1024,640]{1,0:T(8,128)(2,1)} %tok.7, bf16[1024,640]{1,0:T(8,128)(2,1)} %out_grad.3, bf16[1024,640]{1,0:T(8,128)(2,1)} %copy-done, bf16[1024,640]{1,0:T(8,128)(2,1)} %copy-done.18, ...), custom_call_target="tpu_custom_call" | custom-call | flops 5033164800 | bytes 12856320 | tf_op jit(solution)/shard_map/attend_back/pallas_call | solution.py:241
  125.1 0.2 dynamic-update-slice
  125.4 0.2 dynamic-update-slice.1
  125.6 0.2 dynamic-update-slice.2
  125.8 0.2 dynamic-update-slice.3
  126.0 0.2 dynamic-update-slice.4
  126.2 0.4 dynamic-update-slice.5
  126.6 1.4 fusion.3
  128.0 0.1 pad_maximum_fusion
  128.1 0.1 copy.37
  128.2 1.1 copy-done.24
  129.3 35.3 %exchange3.1 = (bf16[1024,640]{1,0:T(8,128)(2,1)S(1)}, f32[80,512]{1,0:T(8,128)S(1)}, f32[96,512]{1,0:T(8,128)S(1)}) custom-call(bf16[1024,640]{1,0:T(8,128)(2,1)S(1)} %copy-done.24, bf16[8,80,512]{2,1,0:T(8,128)(2,1)S(1)} %bitcast.32, bf16[8,96,512]{2,1,0:T(8,128)(2,1)S(1)} %bitcast.31), custom_call_target="tpu_custom_call" | custom-call | flops 6710886400 | bytes 2621440 | tf_op jit(solution)/shard_map/exchange3/pallas_call | solution.py:413
  164.6 0.0 copy-start.1
  164.6 0.0 collective-permute-done
  164.7 1.9 convert_add_fusion.1
  166.6 1.3 copy-done.35
  167.9 0.1 fusion
  167.9 0.1 collective-permute-start.1
  168.0 0.6 fusion.7
  168.6 3.4 %convert_add_fusion = f32[1024,640]{1,0:T(8,128)} fusion(bf16[1024,640]{1,0:T(8,128)(2,1)S(1)} %get-tuple-element.55, bf16[1024,640]{1,0:T(8,128)(2,1)S(1)} %copy-done.1, bf16[1024,640]{1,0:T(8,128)(2,1)} %out_grad.3), kind=kLoop, calls=%fused_computation.1 | loop fusion | flops 3276800 | bytes 6553600 | tf_op jit(solution)/shard_map/add | solution.py:555
  172.0 10.1 %collective-permute-done.1 = bf16[2,80,1536]{2,1,0:T(8,128)(2,1)} collective-permute-done((bf16[2,80,1536]{2,1,0:T(8,128)(2,1)S(1)}, bf16[2,80,1536]{2,1,0:T(8,128)(2,1)}, u32[]{:S(2)}, u32[]{:S(2)}) %collective-permute-start.1) | collective-permute-done | bytes 491552 | tf_op jit(solution)/shard_map/ppermute | solution.py:442
  182.0 1.1 bitcast_add_fusion
  183.2 1.5 collective-permute-start.2
  184.7 0.6 fusion.8
  185.3 0.7 fusion.5
  186.0 10.9 %collective-permute-done.2 = bf16[1,80,1536]{2,1,0:T(8,128)(2,1)S(1)} collective-permute-done((bf16[1,80,1536]{2,1,0:T(8,128)(2,1)S(1)}, bf16[1,80,1536]{2,1,0:T(8,128)(2,1)S(1)}, u32[]{:S(2)}, u32[]{:S(2)}) %collective-permute-start.2) | collective-permute-done | bytes 245792 | tf_op jit(solution)/shard_map/ppermute | solution.py:442
  197.0 0.8 fusion.4
  (71 shorter events, 0.4 us)
Async XLA Ops:
  0.6 4.3 %copy-start.16 = (f32[256]{0:T(256)S(1)}, f32[256]{0:T(256)}, u32[]{:S(2)}) copy-start(f32[256]{0:T(256)} %param.22) | copy-start | bytes 3076
  0.7 4.3 %copy-start.17 = (f32[256]{0:T(256)S(1)}, f32[256]{0:T(256)}, u32[]{:S(2)}) copy-start(f32[256]{0:T(256)} %param.23) | copy-start | bytes 3076
  0.7 4.3 %copy-start.9 = (bf16[640,256]{1,0:T(8,128)(2,1)S(1)}, bf16[640,256]{1,0:T(8,128)(2,1)}, u32[]{:S(2)}) copy-start(bf16[640,256]{1,0:T(8,128)(2,1)} %q_w.3) | copy-start | bytes 983044
  0.7 4.3 %copy-start.10 = (bf16[640,256]{1,0:T(8,128)(2,1)S(1)}, bf16[640,256]{1,0:T(8,128)(2,1)}, u32[]{:S(2)}) copy-start(bf16[640,256]{1,0:T(8,128)(2,1)} %k_w.3) | copy-start | bytes 983044
  0.7 4.3 %copy-start.12 = (bf16[640,256]{1,0:T(8,128)(2,1)S(1)}, bf16[640,256]{1,0:T(8,128)(2,1)}, u32[]{:S(2)}) copy-start(bf16[640,256]{1,0:T(8,128)(2,1)} %v_w.3) | copy-start | bytes 983044
  0.7 4.3 %copy-start.14 = (bf16[640,256]{1,0:T(8,128)(2,1)S(1)}, bf16[640,256]{1,0:T(8,128)(2,1)}, u32[]{:S(2)}) copy-start(bf16[640,256]{1,0:T(8,128)(2,1)} %o_w.3) | copy-start | bytes 983044
  13.9 1.0 copy-start.25
  14.9 1.0 copy-start.27
  15.8 0.8 copy-start.29
  16.6 0.8 copy-start.31
  17.4 0.8 copy-start.33
  18.2 1.3 copy-start.23
  19.5 20.7 %copy-start.37 = (f32[640]{0:T(1024)S(1)}, f32[640]{0:T(1024)}, u32[]{:S(2)}) copy-start(f32[640]{0:T(1024)} %param.25) | copy-start | bytes 7684
  19.5 20.7 %copy-start.38 = (f32[640]{0:T(1024)S(1)}, f32[640]{0:T(1024)}, u32[]{:S(2)}) copy-start(f32[640]{0:T(1024)} %param.26) | copy-start | bytes 7684
  19.5 20.8 %copy-start.2 = (bf16[1024,640]{1,0:T(8,128)(2,1)S(1)}, bf16[1024,640]{1,0:T(8,128)(2,1)}, u32[]{:S(2)}) copy-start(bf16[1024,640]{1,0:T(8,128)(2,1)} %tok.7) | copy-start | bytes 3932164
  19.5 20.8 %copy-start.3 = (bf16[640,512]{1,0:T(8,128)(2,1)S(1)}, bf16[640,512]{1,0:T(8,128)(2,1)}, u32[]{:S(2)}) copy-start(bf16[640,512]{1,0:T(8,128)(2,1)} %gate_w.3) | copy-start | bytes 1966084
  19.5 20.8 %copy-start.5 = (bf16[640,512]{1,0:T(8,128)(2,1)S(1)}, bf16[640,512]{1,0:T(8,128)(2,1)}, u32[]{:S(2)}) copy-start(bf16[640,512]{1,0:T(8,128)(2,1)} %up_w.3) | copy-start | bytes 1966084
  19.5 20.8 %copy-start.7 = (bf16[640,512]{1,0:T(8,128)(2,1)S(1)}, bf16[640,512]{1,0:T(8,128)(2,1)}, u32[]{:S(2)}) copy-start(bf16[640,512]{1,0:T(8,128)(2,1)} %down_w.3) | copy-start | bytes 1966084
  40.2 5.4 %copy-start.18 = (bf16[1024,640]{1,0:T(8,128)(2,1)}, bf16[1024,640]{1,0:T(8,128)(2,1)S(1)}, u32[]{:S(2)}) copy-start(bf16[1024,640]{1,0:T(8,128)(2,1)S(1)} %exchange0.1.attn_sum) | copy-start | bytes 3932164
  45.6 20.8 %copy-start.39 = (f32[640]{0:T(1024)S(1)}, f32[640]{0:T(1024)}, u32[]{:S(2)}) copy-start(f32[640]{0:T(1024)} %param.30) | copy-start | bytes 7684
  65.2 1.1 copy-start.22
  66.4 1.1 copy-start.4
  67.4 1.1 copy-start.6
  68.5 1.1 copy-start.8
  69.6 1.3 copy-start.19
  83.6 1.1 copy-start.20
  86.8 77.8 %collective-permute-start = (bf16[4,80,1536]{2,1,0:T(8,128)(2,1)}, bf16[4,80,1536]{2,1,0:T(8,128)(2,1)}, u32[]{:S(2)}, u32[]{:S(2)}) collective-permute-start(bf16[4,80,1536]{2,1,0:T(8,128)(2,1)} %dynamic-slice_bitcast_fusion), channel_id=1, source_target_pairs={{0,4},{4,0},{8,12},{12,8},{16,20},{20,16},{24,28},{28,24},{1,5},{5... | collective-permute-start | bytes 2949128 | tf_op jit(solution)/shard_map/ppermute | solution.py:442
  88.8 1.3 copy-start.21
  90.2 20.9 %copy-start.11 = (bf16[640,256]{1,0:T(8,128)(2,1)S(1)}, bf16[640,256]{1,0:T(8,128)(2,1)}, u32[]{:S(2)}) copy-start(bf16[640,256]{1,0:T(8,128)(2,1)} %k_w.3) | copy-start | bytes 983044
  90.2 20.9 %copy-start.13 = (bf16[640,256]{1,0:T(8,128)(2,1)S(1)}, bf16[640,256]{1,0:T(8,128)(2,1)}, u32[]{:S(2)}) copy-start(bf16[640,256]{1,0:T(8,128)(2,1)} %v_w.3) | copy-start | bytes 983044
  90.2 20.9 %copy-start.15 = (bf16[640,256]{1,0:T(8,128)(2,1)S(1)}, bf16[640,256]{1,0:T(8,128)(2,1)}, u32[]{:S(2)}) copy-start(bf16[640,256]{1,0:T(8,128)(2,1)} %o_w.3) | copy-start | bytes 983044
  90.2 20.9 %copy-start.26 = (bf16[1536,256]{1,0:T(8,128)(2,1)S(1)}, bf16[1536,256]{1,0:T(8,128)(2,1)}, u32[]{:S(2)}) copy-start(bf16[1536,256]{1,0:T(8,128)(2,1)} %copy-done.25) | copy-start | bytes 2359300
  90.2 20.9 %copy-start.28 = (bf16[1536,256]{1,0:T(8,128)(2,1)S(1)}, bf16[1536,256]{1,0:T(8,128)(2,1)}, u32[]{:S(2)}) copy-start(bf16[1536,256]{1,0:T(8,128)(2,1)} %copy-done.27) | copy-start | bytes 2359300
  90.2 20.9 %copy-start.30 = (bf16[1024,256]{1,0:T(8,128)(2,1)S(1)}, bf16[1024,256]{1,0:T(8,128)(2,1)}, u32[]{:S(2)}) copy-start(bf16[1024,256]{1,0:T(8,128)(2,1)} %copy-done.29) | copy-start | bytes 1572868
  90.2 20.9 %copy-start.32 = (bf16[1024,256]{1,0:T(8,128)(2,1)S(1)}, bf16[1024,256]{1,0:T(8,128)(2,1)}, u32[]{:S(2)}) copy-start(bf16[1024,256]{1,0:T(8,128)(2,1)} %copy-done.31) | copy-start | bytes 1572868
  90.2 20.9 %copy-start.34 = (f32[1024,128]{1,0:T(8,128)S(1)}, f32[1024,128]{1,0:T(8,128)}, u32[]{:S(2)}) copy-start(f32[1024,128]{1,0:T(8,128)} %copy-done.33) | copy-start | bytes 1572868
  110.0 1.1 copy-start
  128.0 1.3 copy-start.24
  164.6 4.0 %copy-start.1 = (bf16[1024,640]{1,0:T(8,128)(2,1)S(1)}, bf16[1024,640]{1,0:T(8,128)(2,1)}, u32[]{:S(2)}) copy-start(bf16[1024,640]{1,0:T(8,128)(2,1)} %copy-done) | copy-start | bytes 3932164
  166.5 1.3 copy-start.35
  167.9 14.1 %collective-permute-start.1 = (bf16[2,80,1536]{2,1,0:T(8,128)(2,1)S(1)}, bf16[2,80,1536]{2,1,0:T(8,128)(2,1)}, u32[]{:S(2)}, u32[]{:S(2)}) collective-permute-start(bf16[2,80,1536]{2,1,0:T(8,128)(2,1)S(1)} %fusion), channel_id=1, source_target_pairs={{0,8},{4,12},{8,0},{12,4},{16,24},{20,28},{24,16},{28,20},{1,9},{5... | collective-permute-start | bytes 1474568 | tf_op jit(solution)/shard_map/ppermute | solution.py:442
  168.6 13.4 %copy-start.36 = (f32[4,80,1536]{2,1,0:T(8,128)S(1)}, f32[4,80,1536]{2,1,0:T(8,128)}, u32[]{:S(2)}) copy-start(f32[4,80,1536]{2,1,0:T(8,128)} %copy-done.35) | copy-start | bytes 5898244
  183.2 13.7 %collective-permute-start.2 = (bf16[1,80,1536]{2,1,0:T(8,128)(2,1)S(1)}, bf16[1,80,1536]{2,1,0:T(8,128)(2,1)S(1)}, u32[]{:S(2)}, u32[]{:S(2)}) collective-permute-start(bf16[1,80,1536]{2,1,0:T(8,128)(2,1)S(1)} %dynamic-slice_convert_fusion.1), channel_id=1, source_target_pairs={{0,16},{4,20},{8,24},{12,28},{16,0},{20,4},{24,8},{28,12},{1,17},{... | collective-permute-start | bytes 737288 | tf_op jit(solution)/shard_map/ppermute | solution.py:442

commit v2 on v1

--- a/solution.py
+++ b/solution.py
@@ -250,14 +250,10 @@
             scratch_shapes=scratch,
         ),
         compiler_params=pltpu.CompilerParams(
-            dimension_semantics=("arbitrary",), vmem_limit_bytes=48 * 1024 * 1024
+            dimension_semantics=("arbitrary",), vmem_limit_bytes=32 * 1024 * 1024
         ),
         cost_estimate=pl.CostEstimate(flops=flops, bytes_accessed=moved, transcendentals=0),
     )(*row_args, *full_args)
-
-
-def flip_pairs(size, bit):
-    return [(index, index ^ bit) for index in range(size)]
 
 
 def flip(index, bit):
@@ -277,7 +273,7 @@
     return copy
 
 
-def exchange_kernel(chunks, orders, *refs):
+def exchange_kernel(chunks, orders, closing, *refs):
     count = len(orders)
     term, blocks, refs = refs[0], refs[1 : 1 + count], refs[1 + count :]
     total, reduced, refs = refs[0], refs[1 : 1 + count], refs[1 + count :]
@@ -289,10 +285,11 @@
     diagonal = flip(y_peer, 1)
     barrier = pltpu.get_barrier_semaphore()
     greeted = [{"tensor": core_peer}, {"tensor": y_peer}]
+    if closing:
+        greeted.append({"tensor": diagonal})
     if count:
         spot = lax.axis_index("dp")
-        greeted.append({"tensor": diagonal})
-        greeted += [{"dp": flip(spot, bit)} for bit in sorted(orders[0])]
+        greeted += [{"dp": flip(spot, bit)} for bit in sorted(set(sum(orders, ())))]
     for device in greeted:
         pl.semaphore_signal(
             barrier, inc=1, device_id=device, device_id_type=pl.DeviceIdType.MESH
@@ -315,11 +312,18 @@
     state = []
     if count:
         scatter_sems = scatter_refs[-1]
-        depth = len(orders[0])
-        slot = 0
+        slots = 0
+        used = 0
         for g, order in enumerate(orders):
-            own = scatter_refs[g * 2 * depth : (g + 1) * 2 * depth]
-            state.append({"order": order, "got": own[:depth], "kept": own[depth:], "src": blocks[g]})
+            depth = len(order)
+            got = scatter_refs[used : used + depth]
+            kept = scatter_refs[used + depth : used + 2 * depth]
+            used += 2 * depth
+            state.append(
+                {"depth": depth, "order": order, "got": got, "kept": kept, "src": blocks[g], "slot": slots}
+            )
+            slots += depth
+        deepest = max(len(order) for order in orders)
 
         def start_stage(g, stage):
             entry = state[g]
@@ -330,7 +334,7 @@
                 entry["src"].at[pl.ds((1 - mine) * width, width)],
                 entry["got"][stage],
                 scatter_sems,
-                g * depth + stage,
+                entry["slot"] + stage,
                 {"dp": flip(spot, bit)},
             )
             copies.append(entry["copy"])
@@ -343,9 +347,14 @@
             for item in range(width):
                 added = entry["src"][mine * width + item].astype(F32)
                 added = added + entry["got"][stage][item].astype(F32)
-                if stage == depth - 1:
+                if stage < entry["depth"] - 1:
+                    entry["kept"][stage][item] = added.astype(BF16)
+                elif not closing:
+                    reduced[g][item] = added.astype(BF16)
+                elif g < count - 1:
                     reduced[g][...] = added
-                entry["kept"][stage][item] = added.astype(BF16)
+                else:
+                    entry["kept"][stage][item] = added.astype(BF16)
             entry["src"] = entry["kept"][stage]
 
         for g in range(count):
@@ -360,7 +369,7 @@
     if count:
         for g in range(count):
             finish_stage(g, 0)
-            if depth > 1:
+            if state[g]["depth"] > 1:
                 start_stage(g, 1)
     third = []
     for c in range(chunks):
@@ -369,22 +378,23 @@
         total[mine, :] = (y_sent[c].astype(F32) + y_got[c].astype(F32)).astype(BF16)
         third.append(send(total.at[mine], back_got.at[c], sems, 2 * chunks + c, {"tensor": core_peer}))
     copies += third
-    for stage in range(1, depth if count else 1):
+    for stage in range(1, deepest if count else 1):
         for g in range(count):
-            finish_stage(g, stage)
-            if stage + 1 < depth:
+            if stage < state[g]["depth"]:
+                finish_stage(g, stage)
+            if stage + 1 < state[g]["depth"]:
                 start_stage(g, stage + 1)
-    if count:
+    if closing:
         shared, shared_got = state[-1]["kept"][-1], scatter_refs[-2]
         final = [
-            send(shared.at[0], shared_got.at[d], scatter_sems, count * depth + d, {"tensor": peer})
+            send(shared.at[0], shared_got.at[d], scatter_sems, slots + d, {"tensor": peer})
             for d, peer in enumerate((core_peer, y_peer, diagonal))
         ]
         copies += final
     for c in range(chunks):
         third[c].wait_recv()
         total[rows(1 - low, c), :] = back_got[c]
-    if count:
+    if closing:
         for copy in final:
             copy.wait_recv()
         pair = shared[0].astype(F32) + shared_got[0].astype(F32)
@@ -393,7 +403,7 @@
         copy.wait_send()
 
 
-def sum_tensor(term, tensor_size, collective, blocks=(), orders=()):
+def sum_tensor(term, tensor_size, collective, blocks=(), orders=(), closing=False):
     assert tensor_size == 4
     tok_count, model = term.shape
     chunks = 4
@@ -402,47 +412,32 @@
     scratch = buffers + [pltpu.SemaphoreType.DMA((2, 3 * chunks))]
     outs = [jax.ShapeDtypeStruct(term.shape, BF16)]
     if blocks:
-        depth = len(orders[0])
-        for part in blocks:
+        for part, order in zip(blocks, orders):
             block = part.shape[1:]
-            widths = [part.shape[0] >> (stage + 1) for stage in range(depth)]
+            widths = [part.shape[0] >> (stage + 1) for stage in range(len(order))]
             scratch += [pltpu.VMEM((width,) + block, BF16) for width in widths] * 2
-            outs.append(jax.ShapeDtypeStruct(block, F32))
-        scratch.append(pltpu.VMEM((3,) + blocks[-1].shape[1:], BF16))
-        scratch.append(pltpu.SemaphoreType.DMA((2, len(blocks) * depth + 3)))
+            shape = block if closing else (widths[-1],) + block
+            outs.append(jax.ShapeDtypeStruct(shape, F32 if closing else BF16))
+        if closing:
+            scratch.append(pltpu.VMEM((3,) + blocks[-1].shape[1:], BF16))
+        slots = sum(len(order) for order in orders) + (3 if closing else 0)
+        scratch.append(pltpu.SemaphoreType.DMA((2, slots)))
     result = pl.pallas_call(
-        functools.partial(exchange_kernel, chunks, orders),
+        functools.partial(exchange_kernel, chunks, orders, closing),
         name="exchange%d" % collective,
         out_shape=tuple(outs),
         in_specs=[pl.BlockSpec(memory_space=pltpu.VMEM)] * (1 + len(blocks)),
         out_specs=tuple(pl.BlockSpec(memory_space=pltpu.VMEM) for _ in outs),
         scratch_shapes=scratch,
         compiler_params=pltpu.CompilerParams(
-            collective_id=collective, has_side_effects=True, vmem_limit_bytes=40 * 1024 * 1024
+            collective_id=collective, has_side_effects=True,
+            vmem_limit_bytes=(24 if blocks else 10) * 1024 * 1024
         ),
         cost_estimate=pl.CostEstimate(
             flops=16 * tok_count * model * 640, bytes_accessed=4 * term.size, transcendentals=0
         ),
     )(term, *blocks)
     return result if blocks else result[0]
-
-
-def scatter_dp(blocks, size):
-    index = lax.axis_index("dp")
-    rows, cols = blocks.shape[1:]
-    total = blocks
-    bit = 1
-    while bit < size:
-        low = lax.rem(lax.div(index, bit), 2)
-        parts = total.reshape(-1, 2, rows, cols)
-        sent = lax.optimization_barrier(
-            lax.dynamic_index_in_dim(parts, 1 - low, 1, keepdims=False).astype(jnp.bfloat16)
-        )
-        kept = lax.dynamic_index_in_dim(parts, low, 1, keepdims=False)
-        got = lax.ppermute(sent, "dp", flip_pairs(size, bit))
-        total = kept.astype(jnp.float32) + got.astype(jnp.float32)
-        bit *= 2
-    return total.reshape(rows, cols)
 
 
 def on_device(
@@ -512,8 +507,22 @@
         (pltpu.VMEM((model, 3 * units), F32),), 24 * square, False,
     )
     part_rows = model // dp_size
-    early = scatter_dp(early.reshape(dp_size, part_rows, 3 * units), dp_size)
-    ffn_back = sum_tensor(term, tensor_size, 2)
+    bits = dp_size.bit_length() - 1
+    plain = tuple(1 << k for k in range(bits))
+    orders = (plain, plain[1::-1] + plain[2:])
+
+    def ordered(part, order):
+        shape = (2,) * bits + part.shape[1:]
+        axes = tuple(bits - bit.bit_length() for bit in order) + (bits, bits + 1)
+        return part.reshape(shape).transpose(axes).reshape(part.shape)
+
+    early = early.reshape(dp_size, part_rows, 3 * units)
+    side = 3 * units // 2
+    ffn_back, early_a, early_b = sum_tensor(
+        term, tensor_size, 2,
+        (ordered(early[:, :, :side], orders[0]), ordered(early[:, :, side:], orders[1])),
+        (orders[0][:2], orders[1][:2]),
+    )
     term, late, attn_gains, head_gains = row_call(
         attend_back_kernel, "attend_back", steps,
         (tokens, out_grad, ffn_back, attn_sum, attn, q_rot, stats, q_unit, k_unit, cosine, sine_tab, low),
@@ -538,20 +547,17 @@
     gains = jnp.pad(gains, (0, gain_rows * cols - gain_count)).reshape(1, gain_rows, cols)
     gains = jnp.broadcast_to(gains.astype(BF16), (dp_size, gain_rows, cols))
     late = late.reshape(dp_size, part_rows, 2 * cols)
-    bits = dp_size.bit_length() - 1
-    plain = tuple(1 << k for k in range(bits))
-    orders = (plain, plain[1::-1] + plain[2:])
-
-    def ordered(part, order):
-        shape = (2,) * bits + part.shape[1:]
-        axes = tuple(bits - bit.bit_length() for bit in order) + (bits, bits + 1)
-        return part.reshape(shape).transpose(axes).reshape(part.shape)
-
     blocks = (
+        early_a,
+        early_b,
         ordered(late[:, :, :cols], orders[0]),
         ordered(jnp.concatenate([late[:, :, cols:], gains], axis=1), orders[1]),
     )
-    attn_back, first_part, shared = sum_tensor(term, tensor_size, 3, blocks, orders)
+    tails = (plain[2:], plain[2:]) + orders
+    attn_back, early_a, early_b, first_part, shared = sum_tensor(
+        term, tensor_size, 3, blocks, tails, True
+    )
+    early = jnp.concatenate([early_a, early_b], axis=1)
     grad_tokens = out_grad.astype(F32) + ffn_back.astype(F32) + attn_back.astype(F32)
     grad_o_w = first_part[:, :head_dim]
     grad_q_w = first_part[:, head_dim:]

time: 198 us -> 151 us (0.76)
  waiting for transfers between devices: 21 us -> 0 us
  local copies, waits for them, and re-layouts: 26.1 us -> 9.6 us
  starting transfers between devices: 3.57 us -> 0 us
  Pallas kernels: 136 us -> 133 us
  other arithmetic: 9.87 us -> 7.24 us
    ppermute x3 -> x0, waiting for transfers between devices: 21 us -> none  [scatter_dp(): got = lax.ppermute(sent, 'dp', flip_pairs(size, bit))]
    unnamed x87 -> x65, local copies, waits for them, and re-layouts: 18.3 us -> 5.9 us
    pallas_call x4, Pallas kernels: 40.7 us -> 33.5 us  [row_call(): pl.pallas_call(kernel, name=name, out_shape=tuple((jax.ShapeDtypeStruct(s...]
    pallas_call x4, Pallas kernels: 95.4 us -> 99.4 us  [sum_tensor(): pl.pallas_call(functools.partial(exchange_kernel, chunks, orders, closing...]
    ppermute x3 -> x0, starting transfers between devices: 3.57 us -> none  [scatter_dp(): got = lax.ppermute(sent, 'dp', flip_pairs(size, bit))]
    add x2 -> x0, other arithmetic: 3.01 us -> none  [scatter_dp(): total = kept.astype(jnp.float32) + got.astype(jnp.float32)]
    squeeze x1 -> x0, local copies, waits for them, and re-layouts: 2.21 us -> none  [scatter_dp(): lax.dynamic_index_in_dim(parts, 1 - low, 1, keepdims=False)]
  transfers between devices with their start and end apart: 3 -> 0, of which waited for: 2 -> 0; matrix products, arithmetic and copies ran while one was open for 4% -> 0% of each run, Pallas kernels for 35% -> 0%
where the time goes in v2:
time: 151 us
  Pallas kernels  133 us (88%)
  local copies, waits for them, and re-layouts  9.6 us (6%)
  other arithmetic  7.24 us (5%)
    pallas_call x4, Pallas kernels, sum_tensor(): pl.pallas_call(functools.partial(exchange_kernel, chunks, orders, closing...  99.4 us
    pallas_call x4, Pallas kernels, row_call(): pl.pallas_call(kernel, name=name, out_shape=tuple((jax.ShapeDtypeStruct(s...  33.5 us
    unnamed x65, local copies, waits for them, and re-layouts  5.9 us

profile of v2, /device:TPU:0, one launch (start us, length us, event | category | flops | bytes accessed | tf_op | source)
XLA Modules:
  0.0 151.0 jit_solution(7333745218056376025)
XLA Ops:
  0.7 0.0 copy-start.5
  0.7 0.0 copy-start.11
  0.7 0.0 copy-start.13
  0.7 1.4 convert_reduce_fusion
  2.2 1.9 %multiply_sine_fusion = (f32[1024,128]{1,0:T(8,128)S(1)}, f32[1024,128]{1,0:T(8,128)S(1)}) fusion(f32[128]{0:T(128)S(1)} %negate_power_fusion, f32[1024]{0:T(1024)S(1)} %subtract_convert_fusion), kind=kLoop, calls=%fused_computation.3 | loop fusion | flops 131072 | bytes 1053184 | tf_op jit(solution)/shard_map/sin | solution.py:474
  4.1 0.0 copy-start.3
  4.1 1.0 copy.36
  5.1 1.1 add_maximum_fusion.low_b.low
  6.3 0.0 copy-start.15
  6.3 1.0 copy-done.15
  7.3 6.9 %attend.1 = (bf16[1024,640]{1,0:T(8,128)(2,1)S(1)}, bf16[1024,256]{1,0:T(8,128)(2,1)S(1)}, bf16[1024,256]{1,0:T(8,128)(2,1)S(1)}, f32[1024,128]{1,0:T(8,128)S(1)...) custom-call(bf16[1024,640]{1,0:T(8,128)(2,1)S(1)} %copy-done.5, ...), custom_call_target="tpu_custom_call" | custom-call | flops 2348810240 | bytes 3678720 | tf_op jit(solution)/shard_map/attend/pallas_call | solution.py:241
  14.2 0.0 copy-start.26
  14.2 0.0 copy-start.27
  14.2 0.0 copy-start.7
  14.2 0.0 copy-start.8
  14.2 0.0 copy-start.9
  14.2 20.7 %exchange0.1.attn_sum = bf16[1024,640]{1,0:T(8,128)(2,1)S(1)} custom-call(bf16[1024,640]{1,0:T(8,128)(2,1)S(1)} %get-tuple-element.42.refs_0_), custom_call_target="tpu_custom_call" | custom-call | flops 6710886400 | bytes 2621440 | tf_op jit(solution)/shard_map/exchange0/pallas_call | solution.py:425
  34.9 0.0 copy-done.26
  34.9 0.0 copy-done.27
  34.9 0.0 copy-done.7
  34.9 0.0 copy-done.8
  35.0 0.0 copy-done.9
  35.0 4.7 %ffn.1 = (bf16[1024,640]{1,0:T(8,128)(2,1)S(1)}, f32[1024,512]{1,0:T(8,128)S(1)}, f32[1024,512]{1,0:T(8,128)S(1)}) custom-call(bf16[1024,640]{1,0:T(8,128)(2,1)S(1)} %copy-done.5, bf16[1024,640]{1,0:T(8,128)(2,1)S(1)} %exchange0.1.attn_sum, f32[1,640]{1,0:T(1,128)S(1)} %broadcast_in_dim.30.pa_gain, f32[1,640]{1,0:T(1,128)S(1)} %broadcast_in_dim.31.pre_gain, ...), custom_call_target="tpu_custom_call" | custom-call | flops 2013265920 | bytes 4592640 | tf_op jit(solution)/shard_map/ffn/pallas_call | solution.py:241
  39.6 0.0 copy-start.28
  39.7 0.0 copy-start
  39.7 0.0 copy-start.6
  39.7 19.7 %exchange1.1.ffn_sum = bf16[1024,640]{1,0:T(8,128)(2,1)S(1)} custom-call(bf16[1024,640]{1,0:T(8,128)(2,1)S(1)} %get-tuple-element.43.refs_0_), custom_call_target="tpu_custom_call" | custom-call | flops 6710886400 | bytes 2621440 | tf_op jit(solution)/shard_map/exchange1/pallas_call | solution.py:425
  59.4 10.6 %ffn_back.1 = (bf16[1024,640]{1,0:T(8,128)(2,1)}, bf16[1024,640]{1,0:T(8,128)(2,1)S(1)}, bf16[640,1536]{1,0:T(8,128)(2,1)S(1)}, f32[8,640]{1,0:T(8,128)S(1)}) custom-call(bf16[1024,640]{1,0:T(8,128)(2,1)S(1)} %copy-done.6, bf16[1024,640]{1,0:T(8,128)(2,1)S(1)} %exchange0.1.attn_sum, bf16[1024,640]{1,0:T(8,128)(2,1)S(1)} %exchange1.1.ffn_sum, ...), custom_call_target="tpu_custom_call" | custom-call | flops 4026531840 | bytes 11410944 | tf_op jit(solution)/shard_map/ffn_back/pallas_call | solution.py:241
  70.0 0.1 fusion.2
  70.1 0.1 copy.38
  70.2 0.1 copy.37
  70.3 0.0 copy-start.4
  70.3 0.0 copy-start.12
  70.3 0.0 copy-start.14
  70.3 0.0 copy-start.16
  70.3 22.4 %exchange2.1 = (bf16[1024,640]{1,0:T(8,128)(2,1)S(1)}, bf16[2,80,768]{2,1,0:T(8,128)(2,1)S(1)}, bf16[2,80,768]{2,1,0:T(8,128)(2,1)S(1)}) custom-call(bf16[1024,640]{1,0:T(8,128)(2,1)S(1)} %get-tuple-element.47.refs_0_, bf16[8,80,768]{2,1,0:T(8,128)(2,1)S(1)} %bitcast.28, bf16[8,80,768]{2,1,0:T(8,128)(2,1)S(1)} %bitcast.27), custom_call_target="tpu_custom_call" | custom-call | flops 6710886400 | bytes 2621440 | tf_op jit(solution)/shard_map/exchange2/pallas_call | solution.py:425
  92.7 0.7 copy-done.21
  93.4 0.7 copy-done.23
  94.1 0.0 copy-done.12
  94.1 11.4 %attend_back.1 = (bf16[1024,640]{1,0:T(8,128)(2,1)S(1)}, bf16[640,1024]{1,0:T(8,128)(2,1)S(1)}, f32[8,640]{1,0:T(8,128)S(1)}, f32[8,256]{1,0:T(8,128)S(1)}) custom-call(bf16[1024,640]{1,0:T(8,128)(2,1)S(1)} %copy-done.6, bf16[1024,640]{1,0:T(8,128)(2,1)S(1)} %copy-done, bf16[1024,640]{1,0:T(8,128)(2,1)S(1)} %get-tuple-element.49.ffn_back, ...), custom_call_target="tpu_custom_call" | custom-call | flops 5033164800 | bytes 12856320 | tf_op jit(solution)/shard_map/attend_back/pallas_call | solution.py:241
  105.5 0.0 copy-done.1
  105.5 0.0 copy-start.19
  105.5 1.0 copy-done.19
  106.6 0.2 dynamic-update-slice
  106.9 0.2 dynamic-update-slice.1
  107.1 0.2 dynamic-update-slice.2
  107.3 0.2 dynamic-update-slice.3
  107.6 0.2 dynamic-update-slice.4
  107.8 0.2 dynamic-update-slice.5
  108.0 0.1 fusion.3
  108.2 0.1 pad_maximum_fusion
  108.2 0.0 copy-start.20
  108.2 0.0 copy-start.22
  108.3 0.0 copy-start.24
  108.3 0.1 copy.40
  108.4 1.2 copy-done.20
  109.6 0.0 copy-done.22
  109.6 0.1 copy-done.24
  109.7 36.7 %exchange3.1 = (bf16[1024,640]{1,0:T(8,128)(2,1)S(1)}, f32[80,768]{1,0:T(8,128)S(1)}, f32[80,768]{1,0:T(8,128)S(1)}, f32[80,512]{1,0:T(8,128)S(1)}, f32[96,512]{1,0:T(8,128)S(1)}) custom-call(bf16[1024,640]{1,0:T(8,128)(2,1)S(1)} %copy-done.20, bf16[2,80,768]{2,1,0:T(8,128)(2,1)S(1)} %copy-done.22, bf16[2,80,768]{2,1,0:T(8,128)(2,1)S(1)} %copy-done.24, ...), custom_call_target="tpu_custom_call" | custom-call | flops 6710886400 | bytes 2621440 | tf_op jit(solution)/shard_map/exchange3/pallas_call | solution.py:425
  146.3 0.8 fusion.4
  147.1 0.7 fusion.5
  147.8 1.9 %convert_add_fusion = f32[1024,640]{1,0:T(8,128)} fusion(bf16[1024,640]{1,0:T(8,128)(2,1)S(1)} %get-tuple-element.64, bf16[1024,640]{1,0:T(8,128)(2,1)S(1)} %copy-done.2, bf16[1024,640]{1,0:T(8,128)(2,1)S(1)} %copy-done), kind=kLoop, calls=%fused_computation.1 | loop fusion | flops 3276800 | bytes 6553600 | tf_op jit(solution)/shard_map/add | solution.py:561
  149.8 0.6 fusion.7
  150.4 0.6 fusion.8
  (40 shorter events, 0.3 us)
Async XLA Ops:
  0.6 5.6 %copy-start.25 = (f32[640]{0:T(1024)S(1)}, f32[640]{0:T(1024)}, u32[]{:S(2)}) copy-start(f32[640]{0:T(1024)} %param.18) | copy-start | bytes 7684
  0.7 5.6 %copy-start.17 = (f32[256]{0:T(256)S(1)}, f32[256]{0:T(256)}, u32[]{:S(2)}) copy-start(f32[256]{0:T(256)} %param.22) | copy-start | bytes 3076
  0.7 5.6 %copy-start.18 = (f32[256]{0:T(256)S(1)}, f32[256]{0:T(256)}, u32[]{:S(2)}) copy-start(f32[256]{0:T(256)} %param.23) | copy-start | bytes 3076
  0.7 5.6 %copy-start.5 = (bf16[1024,640]{1,0:T(8,128)(2,1)S(1)}, bf16[1024,640]{1,0:T(8,128)(2,1)}, u32[]{:S(2)}) copy-start(bf16[1024,640]{1,0:T(8,128)(2,1)} %tok.7) | copy-start | bytes 3932164
  0.7 5.6 %copy-start.10 = (bf16[640,256]{1,0:T(8,128)(2,1)S(1)}, bf16[640,256]{1,0:T(8,128)(2,1)}, u32[]{:S(2)}) copy-start(bf16[640,256]{1,0:T(8,128)(2,1)} %q_w.3) | copy-start | bytes 983044
  0.7 5.6 %copy-start.11 = (bf16[640,256]{1,0:T(8,128)(2,1)S(1)}, bf16[640,256]{1,0:T(8,128)(2,1)}, u32[]{:S(2)}) copy-start(bf16[640,256]{1,0:T(8,128)(2,1)} %k_w.3) | copy-start | bytes 983044
  0.7 5.6 %copy-start.13 = (bf16[640,256]{1,0:T(8,128)(2,1)S(1)}, bf16[640,256]{1,0:T(8,128)(2,1)}, u32[]{:S(2)}) copy-start(bf16[640,256]{1,0:T(8,128)(2,1)} %v_w.3) | copy-start | bytes 983044
  4.1 10.1 %copy-start.3 = (f32[1024,128]{1,0:T(8,128)}, f32[1024,128]{1,0:T(8,128)S(1)}, u32[]{:S(2)}) copy-start(f32[1024,128]{1,0:T(8,128)S(1)} %get-tuple-element.93.cos_b.cosine) | copy-start | bytes 1572868
  6.3 1.0 copy-start.15
  14.2 20.7 %copy-start.26 = (f32[640]{0:T(1024)S(1)}, f32[640]{0:T(1024)}, u32[]{:S(2)}) copy-start(f32[640]{0:T(1024)} %param.25) | copy-start | bytes 7684
  14.2 20.8 %copy-start.27 = (f32[640]{0:T(1024)S(1)}, f32[640]{0:T(1024)}, u32[]{:S(2)}) copy-start(f32[640]{0:T(1024)} %param.26) | copy-start | bytes 7684
  14.2 20.8 %copy-start.7 = (bf16[640,512]{1,0:T(8,128)(2,1)S(1)}, bf16[640,512]{1,0:T(8,128)(2,1)}, u32[]{:S(2)}) copy-start(bf16[640,512]{1,0:T(8,128)(2,1)} %gate_w.3) | copy-start | bytes 1966084
  14.2 20.8 %copy-start.8 = (bf16[640,512]{1,0:T(8,128)(2,1)S(1)}, bf16[640,512]{1,0:T(8,128)(2,1)}, u32[]{:S(2)}) copy-start(bf16[640,512]{1,0:T(8,128)(2,1)} %up_w.3) | copy-start | bytes 1966084
  14.2 20.8 %copy-start.9 = (bf16[640,512]{1,0:T(8,128)(2,1)S(1)}, bf16[640,512]{1,0:T(8,128)(2,1)}, u32[]{:S(2)}) copy-start(bf16[640,512]{1,0:T(8,128)(2,1)} %down_w.3) | copy-start | bytes 1966084
  39.6 19.7 %copy-start.28 = (f32[640]{0:T(1024)S(1)}, f32[640]{0:T(1024)}, u32[]{:S(2)}) copy-start(f32[640]{0:T(1024)} %param.30) | copy-start | bytes 7684
  39.7 19.7 %copy-start = (bf16[1024,640]{1,0:T(8,128)(2,1)S(1)}, bf16[1024,640]{1,0:T(8,128)(2,1)}, u32[]{:S(2)}) copy-start(bf16[1024,640]{1,0:T(8,128)(2,1)} %out_grad.3) | copy-start | bytes 3932164
  39.7 19.7 %copy-start.6 = (bf16[1024,640]{1,0:T(8,128)(2,1)S(1)}, bf16[1024,640]{1,0:T(8,128)(2,1)}, u32[]{:S(2)}) copy-start(bf16[1024,640]{1,0:T(8,128)(2,1)} %tok.7) | copy-start | bytes 3932164
  70.3 23.8 %copy-start.4 = (f32[1024,128]{1,0:T(8,128)S(1)}, f32[1024,128]{1,0:T(8,128)}, u32[]{:S(2)}) copy-start(f32[1024,128]{1,0:T(8,128)} %copy-done.3) | copy-start | bytes 1572868
  70.3 23.8 %copy-start.12 = (bf16[640,256]{1,0:T(8,128)(2,1)S(1)}, bf16[640,256]{1,0:T(8,128)(2,1)}, u32[]{:S(2)}) copy-start(bf16[640,256]{1,0:T(8,128)(2,1)} %k_w.3) | copy-start | bytes 983044
  70.3 23.8 %copy-start.14 = (bf16[640,256]{1,0:T(8,128)(2,1)S(1)}, bf16[640,256]{1,0:T(8,128)(2,1)}, u32[]{:S(2)}) copy-start(bf16[640,256]{1,0:T(8,128)(2,1)} %v_w.3) | copy-start | bytes 983044
  70.3 23.8 %copy-start.16 = (bf16[640,256]{1,0:T(8,128)(2,1)S(1)}, bf16[640,256]{1,0:T(8,128)(2,1)}, u32[]{:S(2)}) copy-start(bf16[640,256]{1,0:T(8,128)(2,1)} %o_w.3) | copy-start | bytes 983044
  92.7 0.7 copy-start.21
  93.4 0.7 copy-start.23
  94.1 11.4 %copy-start.1 = (bf16[1024,640]{1,0:T(8,128)(2,1)}, bf16[1024,640]{1,0:T(8,128)(2,1)S(1)}, u32[]{:S(2)}) copy-start(bf16[1024,640]{1,0:T(8,128)(2,1)S(1)} %get-tuple-element.49.ffn_back) | copy-start | bytes 3932164
  105.5 1.1 copy-start.19
  108.2 1.3 copy-start.20
  108.2 1.3 copy-start.22
  108.3 1.4 copy-start.24
  146.3 1.5 %copy-start.2 = (bf16[1024,640]{1,0:T(8,128)(2,1)S(1)}, bf16[1024,640]{1,0:T(8,128)(2,1)}, u32[]{:S(2)}) copy-start(bf16[1024,640]{1,0:T(8,128)(2,1)} %copy-done.1) | copy-start | bytes 3932164
